TPU v7x, 256 devices: a whole 4x4x8 slice. The times are simulated.
256 devices in a mesh: inner: 16 (over x, y), outer: 16 (over z, core).
Axes of the slice: x: 4, y: 4, z: 8, core: 2. Of those that a mesh axis runs over, the one named last changes fastest.
Arguments:
- tokens: int32 [4096], P('outer'), may hold values from 0 to 16383
- step_index: int32 [1], replicated, may hold values from 0 to 31
- embed_table: bfloat16 [16384, 2048], P(None, 'inner'), may hold values from -6 to 6
- gain_one: float32 [2048], replicated, may hold values from 0.5 to 1.5
- gate_weight: bfloat16 [2048, 5632], P(None, 'inner'), may hold values from -0.125 to 0.125
- up_weight: bfloat16 [2048, 5632], P(None, 'inner'), may hold values from -0.125 to 0.125
- down_weight: bfloat16 [5632, 2048], P('inner'), may hold values from -0.078125 to 0.078125
- gain_two: float32 [2048], replicated, may hold values from 0.5 to 1.5
- query_weight: bfloat16 [2048, 2048], P(None, 'inner'), may hold values from -0.125 to 0.125
- key_weight: bfloat16 [2048, 2048], P(None, 'inner'), may hold values from -0.125 to 0.125
- value_weight: bfloat16 [2048, 4096], P(None, 'inner'), may hold values from -0.125 to 0.125
- decay_weight: bfloat16 [2048, 16], P(None, 'inner'), may hold values from -0.125 to 0.125
- beta_weight: bfloat16 [2048, 16], P(None, 'inner'), may hold values from -0.125 to 0.125
- rate_log: float32 [16], P('inner'), may hold values from -12 to -2
- decay_bias: float32 [16], P('inner'), may hold values from -1 to 1
- beta_bias: float32 [16], P('inner'), may hold values from -6 to -2
- cotangent: bfloat16 [4096, 4096], P('outer', 'inner'), may hold values from -192 to 192
Outputs:
- attribution: float32 [4096, 5632], P('outer', 'inner')
All inputs are finite; a program needn't handle non-finite values.
Results may differ from a plain program's by a relative error of at most 0.029.
Values may be sent and summed in bfloat16 or wider, within the bound.
A program may use at most 128 MiB of HBM per device.

v0:
```python
import functools
import math

import jax
import jax.numpy as jnp
from jax import lax
from jax.sharding import PartitionSpec as P

STEPS = 32


def from_behind(array, axis, by):
    devices = lax.axis_size(axis)
    pairs = [(i, i + by) for i in range(devices) if 0 <= i + by < devices]
    return lax.ppermute(array, axis, pairs)


def unit_rows(values):
    return values * lax.rsqrt(jnp.sum(values * values, axis=-1, keepdims=True) + 1e-06)


def head_inputs(query_rows, key_rows, decay_rows, beta_rows, log_rate, rate_shift, beta_shift):
    queries = unit_rows(query_rows) * query_rows.shape[-1] ** (-0.5)
    keys_unit = unit_rows(key_rows)
    log_decay = -jnp.exp(log_rate) * jax.nn.softplus(decay_rows + rate_shift)
    betas = jax.nn.sigmoid(beta_rows + beta_shift)
    return (queries, keys_unit, log_decay, betas)


def block_step(with_out, state, pieces):
    queries, keys_unit, values, log_decay, betas = pieces
    block_len = keys_unit.shape[0]
    highest = lax.Precision.HIGHEST
    cum_decay = jnp.cumsum(log_decay)
    row_ids = jnp.arange(block_len)[:, None]
    col_ids = jnp.arange(block_len)[None, :]
    lower_mask = row_ids >= col_ids
    decay_mat = jnp.where(
        lower_mask,
        jnp.exp(jnp.where(lower_mask, cum_decay[:, None] - cum_decay[None, :], 0.0)),
        0.0,
    )
    key_gram = jnp.dot(keys_unit, keys_unit.T, precision=highest)
    strict = jnp.where(row_ids > col_ids, betas[:, None] * decay_mat * key_gram, 0.0)
    system = strict + jnp.eye(block_len, dtype=jnp.float32)
    start_scale = jnp.exp(cum_decay)[:, None]
    target = betas[:, None] * (values - start_scale * jnp.dot(keys_unit, state, precision=highest))
    fresh_vals = lax.linalg.triangular_solve(
        system, target, left_side=True, lower=True, unit_diagonal=True
    )
    tail_keys = jnp.exp(cum_decay[-1] - cum_decay)[:, None] * keys_unit
    new_state = jnp.exp(cum_decay[-1]) * state + jnp.dot(tail_keys.T, fresh_vals, precision=highest)
    if with_out:
        scores = decay_mat * jnp.dot(queries, keys_unit.T, precision=highest)
        output = start_scale * jnp.dot(queries, state, precision=highest) + jnp.dot(
            scores, fresh_vals, precision=highest
        )
        return (new_state, output)
    return (new_state, None)


def run_blocks(queries, keys_unit, values, log_decay, betas, state, with_out):
    length = keys_unit.shape[0]
    block_len = math.gcd(64, length)
    block_count = length // block_len

    def blocked(array):
        return array.reshape((block_count, block_len) + array.shape[1:])

    step_fn = functools.partial(block_step, with_out)
    final_state, outputs = lax.scan(
        step_fn,
        state,
        (blocked(queries), blocked(keys_unit), blocked(values), blocked(log_decay), blocked(betas)),
    )
    if with_out:
        outputs = outputs.reshape((length,) + outputs.shape[2:])
    return (final_state, outputs)


def rms_scaled(values, gain):
    return values * lax.rsqrt(jnp.mean(values * values, axis=-1, keepdims=True) + 1e-06) * gain


def apply_map(matrix, state):
    return jnp.einsum("hij,hjv->hiv", matrix, state, precision=lax.Precision.HIGHEST)


def shards(
    tokens,
    step_index,
    embed_table,
    gain_one,
    gate_weight,
    up_weight,
    down_weight,
    gain_two,
    query_weight,
    key_weight,
    value_weight,
    decay_weight,
    beta_weight,
    rate_log,
    decay_bias,
    beta_bias,
    cotangent,
):
    columns = jnp.take(embed_table, tokens, axis=0)
    embedded = lax.all_gather(columns, "inner", axis=1, tiled=True)
    emb_float = embedded.astype(jnp.float32)
    normed_one = rms_scaled(emb_float, gain_one).astype(jnp.bfloat16)
    gate_rows = jnp.dot(normed_one, gate_weight, preferred_element_type=jnp.float32)
    up_rows = jnp.dot(normed_one, up_weight, preferred_element_type=jnp.float32)
    hidden = jax.nn.silu(gate_rows) * up_rows
    path_scale = (step_index[0].astype(jnp.float32) + 0.5) / STEPS
    scaled = (path_scale * hidden).astype(jnp.bfloat16)
    group_rows = tokens.shape[0]
    row_share = group_rows // lax.axis_size("inner")
    head_count = rate_log.shape[0]
    key_dim = query_weight.shape[1] // head_count
    value_dim = value_weight.shape[1] // head_count
    main_weight = jnp.concatenate([query_weight, key_weight, value_weight], axis=1)
    gate_pair = jnp.concatenate([decay_weight, beta_weight], axis=1)

    def normalize(values):
        return rms_scaled(values, gain_two)

    mixed_share = lax.psum_scatter(
        jnp.dot(scaled, down_weight, preferred_element_type=jnp.float32).astype(jnp.bfloat16),
        "inner",
        scatter_dimension=0,
        tiled=True,
    ).astype(jnp.float32)
    own_rows = lax.dynamic_slice_in_dim(
        emb_float, lax.axis_index("inner") * row_share, row_share, 0
    )
    normed_float, norm_pull = jax.vjp(normalize, own_rows + mixed_share)
    block_piece = lax.all_gather(normed_float.astype(jnp.bfloat16), "inner", axis=0, tiled=True)
    main_part = jnp.dot(block_piece, main_weight, preferred_element_type=jnp.float32)
    gate_part = jnp.dot(block_piece, gate_pair, preferred_element_type=jnp.float32)
    projected = jnp.concatenate([main_part, gate_part], axis=1)
    key_span = head_count * key_dim
    value_span = head_count * value_dim

    def by_head(columns_block, width):
        return columns_block.reshape(group_rows, head_count, width).transpose(1, 0, 2)

    query_pre = by_head(projected[:, :key_span], key_dim)
    key_pre = by_head(projected[:, key_span : 2 * key_span], key_dim)
    value_pre = by_head(projected[:, 2 * key_span : 2 * key_span + value_span], value_dim)
    gate_start = 2 * key_span + value_span
    decay_pre = projected[:, gate_start : gate_start + head_count].T
    beta_pre = projected[:, gate_start + head_count : gate_start + 2 * head_count].T
    cot_heads = by_head(cotangent.astype(jnp.float32), value_dim)

    def carry_map(key_rows, value_rows, decay_rows, beta_rows, log_rate, rate_shift, beta_shift):
        unused_query, keys_unit, log_decay, betas = head_inputs(
            key_rows, key_rows, decay_rows, beta_rows, log_rate, rate_shift, beta_shift
        )
        padded_vals = jnp.concatenate(
            [value_rows, jnp.zeros((key_rows.shape[0], key_dim), jnp.float32)], axis=1
        )
        start_state = jnp.concatenate(
            [jnp.zeros((key_dim, value_dim), jnp.float32), jnp.eye(key_dim, dtype=jnp.float32)],
            axis=1,
        )
        final_state, unused_out = run_blocks(
            keys_unit, keys_unit, padded_vals, log_decay, betas, start_state, False
        )
        return final_state

    joined_state = jax.vmap(carry_map)(
        key_pre, value_pre, decay_pre, beta_pre, rate_log, decay_bias, beta_bias
    )
    offset_state = joined_state[:, :, :value_dim]
    transition = joined_state[:, :, value_dim:]

    def forward_step(turn_index, carried):
        incoming = from_behind(carried[1].astype(jnp.bfloat16), "outer", 1).astype(jnp.float32)
        return (incoming, apply_map(transition, incoming) + offset_state)

    state_in, unused_end = lax.fori_loop(
        0, lax.axis_size("outer") - 1, forward_step, (jnp.zeros_like(offset_state), offset_state)
    )

    def local_score(query_in, key_in, value_in, decay_in, beta_in, start_in):

        def one_head(
            query_rows,
            key_rows,
            value_rows,
            decay_rows,
            beta_rows,
            start_state,
            cot_rows,
            log_rate,
            rate_shift,
            beta_shift,
        ):
            queries, keys_unit, log_decay, betas = head_inputs(
                query_rows, key_rows, decay_rows, beta_rows, log_rate, rate_shift, beta_shift
            )
            final_state, outputs = run_blocks(
                queries, keys_unit, value_rows, log_decay, betas, start_state, True
            )
            return (jnp.sum(outputs * cot_rows), final_state)

        head_scores, final_states = jax.vmap(one_head)(
            query_in,
            key_in,
            value_in,
            decay_in,
            beta_in,
            start_in,
            cot_heads,
            rate_log,
            decay_bias,
            beta_bias,
        )
        return (jnp.sum(head_scores), final_states)

    score_pair, pull_back = jax.vjp(
        local_score, query_pre, key_pre, value_pre, decay_pre, beta_pre, state_in
    )
    first_pull = pull_back((jnp.ones_like(score_pair[0]), jnp.zeros_like(score_pair[1])))
    grad_local = first_pull[5]
    grad_trans = jnp.swapaxes(transition, 1, 2)

    def backward_step(turn_index, carried):
        incoming = from_behind(carried[1].astype(jnp.bfloat16), "outer", -1).astype(jnp.float32)
        return (incoming, apply_map(grad_trans, incoming) + grad_local)

    state_grad, unused_start = lax.fori_loop(
        0, lax.axis_size("outer") - 1, backward_step, (jnp.zeros_like(grad_local), grad_local)
    )
    second_pull = pull_back((jnp.zeros_like(score_pair[0]), state_grad))
    summed = [first_pull[which] + second_pull[which] for which in range(5)]

    def by_rows(head_block):
        return head_block.transpose(1, 0, 2).reshape(group_rows, -1).astype(jnp.bfloat16)

    grad_main = jnp.concatenate(
        [by_rows(summed[0]), by_rows(summed[1]), by_rows(summed[2])], axis=1
    )
    grad_gates = jnp.concatenate(
        [summed[3].T.astype(jnp.bfloat16), summed[4].T.astype(jnp.bfloat16)], axis=1
    )
    main_part = jnp.dot(grad_main, main_weight.T, preferred_element_type=jnp.float32)
    back_share = lax.psum_scatter(
        (main_part + jnp.dot(grad_gates, gate_pair.T, preferred_element_type=jnp.float32)).astype(
            jnp.bfloat16
        ),
        "inner",
        scatter_dimension=0,
        tiled=True,
    ).astype(jnp.float32)
    grad_mixed = norm_pull(back_share)[0].astype(jnp.bfloat16)
    return hidden * jnp.dot(
        lax.all_gather(grad_mixed, "inner", axis=0, tiled=True),
        down_weight.T,
        preferred_element_type=jnp.float32,
    )


def solution(mesh):
    placed = (
        P("outer"),
        P(),
        P(None, "inner"),
        P(),
        P(None, "inner"),
        P(None, "inner"),
        P("inner", None),
        P(),
        P(None, "inner"),
        P(None, "inner"),
        P(None, "inner"),
        P(None, "inner"),
        P(None, "inner"),
        P("inner"),
        P("inner"),
        P("inner"),
        P("outer", "inner"),
    )
    return jax.shard_map(
        shards, mesh=mesh, in_specs=placed, out_specs=P("outer", "inner"), check_vma=False
    )
```

profile of v0, /device:TPU:2, one launch (start us, length us, event | category | flops | bytes accessed | tf_op | source)
XLA Modules:
  0.0 940.5 jit_solution(13554615384378259436)
XLA Ops:
  12.9 50.5 %all-gather.4.cloned.1.call-done = bf16[256,2048]{1,0:T(8,128)(2,1)} async-done(((bf16[256,128]{1,0:T(8,128)(2,1)}), bf16[256,2048]{1,0:T(8,128)(2,1)}) %all-gather.4.cloned.1.call-update) | async-done | bytes 1048592 | tf_op jit(solution)/shard_map/all_gather | solution.py:109
  71.6 75.9 %reduce-scatter.3.cloned.1.call-done = bf16[16,2048]{1,0:T(8,128)(2,1)} async-done(((bf16[256,2048]{1,0:T(8,128)(2,1)}), bf16[16,2048]{1,0:T(8,128)(2,1)}) %reduce-scatter.3.cloned.1.call-update) | async-done | bytes 65552 | tf_op jit(solution)/shard_map/reduce_scatter | solution.py:128
  159.2 38.1 %all-gather.6.cloned.1.call-done = bf16[256,2048]{1,0:T(8,128)(2,1)} async-done(((bf16[16,2048]{1,0:T(8,128)(2,1)}), bf16[256,2048]{1,0:T(8,128)(2,1)}) %all-gather.6.cloned.1.call-update) | async-done | bytes 1048592 | tf_op jit(solution)/shard_map/all_gather | solution.py:138
  207.2 42.2 %while.149 = (s32[]{:T(128)}, f32[1,128,384]{2,1,0:T(8,128)S(1)}, f32[4,1,64]{2,1,0:T(1,128)}, f32[4,1,64,128]{3,2,1,0:T(8,128)S(1)}, f32[4,1,64]{2,1,0:T(1,128)...) while((s32[]{:T(128)}, f32[1,128,384]{2,1,0:T(8,128)S(1)}, f32[4,1,64]{2,1,0:T(1,128)}, ...), condition=%wide.region_6.7_spmd, body=%wide.region_4.6_spmd.sunk | while | flops 100913216 | bytes 1219713 | solution.py:71
  252.5 93.5 %while.150 = (s32[]{:T(128)}, f32[1,128,256]{2,1,0:T(8,128)}, bf16[1,128,256]{2,1,0:T(8,128)(2,1)S(1)}, f32[1,128,128]{2,1,0:T(8,128)S(1)}, f32[1,128,256]{2,1,0:T(8,128)S(1)}, /*index=5*/s32[]{:T(128)}) while((s32[]{:T(128)}, f32[1,128,256]{2,1,0:T(8,128)}, bf16[1,128,256]{2,1,0:T(8,128)(2,1)S(1)}, f32[1,128,128]{2,1,0:T(8,128)S(1)}, ...), condition=%wide.region_8.9_spmd, body=%wide.region_7.8_spmd.sunk | while | flops 50429952 | bytes 786541 | solution.py:182
  348.8 95.0 %while.152 = (s32[]{:T(128)}, f32[1,128,256]{2,1,0:T(8,128)}, f32[4,1,64,64]{3,2,1,0:T(8,128)}, f32[4,1,128,64]{3,2,1,0:T(8,128)}, f32[4,1,64,64]{3,2,1,0:T(8,12...) while((s32[]{:T(128)}, f32[1,128,256]{2,1,0:T(8,128)}, ...), condition=%wide.region_12.13_spmd.clone.clone, body=%wide.region_10.12_spmd.clone.clone.sunk | while | flops 100962496 | bytes 2558033 | solution.py:71
  445.9 108.1 %while.154 = (s32[]{:T(128)}, f32[1,128,256]{1,2,0:T(8,128)S(1)}, f32[4,1,64,128]{3,2,1,0:T(8,128)}, f32[4,1,64,128]{3,2,1,0:T(8,128)}, f32[4,1,64,256]{3,2,1,0:...) while((s32[]{:T(128)}, f32[1,128,256]{1,2,0:T(8,128)S(1)}, ...), condition=%wide.region_24.27_spmd.clone.clone, body=%wide.region_13.26_spmd.clone.clone.sunk | while | flops 230404480 | bytes 3990816 | solution.py:71
  554.8 116.3 %while.151 = (s32[]{:T(128)}, f32[1,128,256]{2,1,0:T(8,128)}, bf16[1,128,256]{2,1,0:T(8,128)(2,1)S(1)}, f32[1,128,128]{2,1,0:T(8,128)S(1)}, f32[1,128,256]{2,1,0:T(8,128)S(1)}, /*index=5*/s32[]{:T(128)}) while((s32[]{:T(128)}, f32[1,128,256]{2,1,0:T(8,128)}, bf16[1,128,256]{2,1,0:T(8,128)(2,1)S(1)}, f32[1,128,128]{2,1,0:T(8,128)S(1)}, ...), condition=%wide.region_27.30_spmd, body=%wide.region_26.29_spmd.sunk | while | flops 50429952 | bytes 786541 | solution.py:233
  562.9 6.1 collective-permute-done.1
  571.2 5.4 collective-permute-done.1
  578.7 6.1 collective-permute-done.1
  587.0 5.4 collective-permute-done.1
  594.6 6.1 collective-permute-done.1
  610.4 6.1 collective-permute-done.1
  618.7 5.5 collective-permute-done.1
  626.4 5.5 collective-permute-done.1
  634.1 5.5 collective-permute-done.1
  641.7 5.5 collective-permute-done.1
  649.4 5.5 collective-permute-done.1
  657.1 5.5 collective-permute-done.1
  664.8 5.5 collective-permute-done.1
  674.3 102.9 %while.153 = (s32[]{:T(128)}, f32[1,128,256]{1,2,0:T(8,128)S(1)}, f32[4,1,64,128]{3,2,1,0:T(8,128)}, f32[4,1,64,128]{3,2,1,0:T(8,128)}, f32[4,1,64,256]{3,2,1,0:...) while((s32[]{:T(128)}, f32[1,128,256]{1,2,0:T(8,128)S(1)}, ...), condition=%wide.region_39.42_spmd.clone.clone, body=%wide.region_28.41_spmd.clone.clone.sunk | while | flops 230273408 | bytes 4006157 | solution.py:71
  786.2 95.3 %reduce-scatter.5.cloned.1.call-done = bf16[16,2048]{1,0:T(8,128)(2,1)} async-done(((bf16[256,2048]{1,0:T(8,128)(2,1)}), bf16[16,2048]{1,0:T(8,128)(2,1)}) %reduce-scatter.5.cloned.1.call-update) | async-done | bytes 65552 | tf_op jit(solution)/shard_map/reduce_scatter | solution.py:249
  884.3 47.1 %all-gather.8.cloned.1.call-done = bf16[256,2048]{1,0:T(8,128)(2,1)} async-done(((bf16[16,2048]{1,0:T(8,128)(2,1)}), bf16[256,2048]{1,0:T(8,128)(2,1)}) %all-gather.8.cloned.1.call-update) | async-done | bytes 1048592 | tf_op jit(solution)/shard_map/all_gather | solution.py:259
  (668 shorter events, 526.0 us)
Async XLA Ops:
  6.5 56.9 %all-gather.4.cloned.1.call-start = ((), (), s32[]{:S(2)}) async-start(), calls=%async_computation.2 | async-start | bytes 1114112 | tf_op jit(solution)/shard_map/all_gather | solution.py:109
  12.2 135.2 %reduce-scatter.3.cloned.1.call-start = ((), (), s32[]{:S(2)}) async-start(), calls=%async_computation.3 | async-start | bytes 1114112 | tf_op jit(solution)/shard_map/reduce_scatter | solution.py:128
  69.9 127.4 %all-gather.6.cloned.1.call-start = ((), (), s32[]{:S(2)}) async-start(), calls=%async_computation.4 | async-start | bytes 1114112 | tf_op jit(solution)/shard_map/all_gather | solution.py:138
  150.2 731.3 %reduce-scatter.5.cloned.1.call-start = ((), (), s32[]{:S(2)}) async-start(), calls=%async_computation.5 | async-start | bytes 1114112 | tf_op jit(solution)/shard_map/reduce_scatter | solution.py:249
  262.0 5.6 collective-permute-start
  287.8 5.6 collective-permute-start
  313.7 5.6 collective-permute-start
  339.6 5.6 collective-permute-start
  554.8 5.9 collective-permute-start.1
  561.6 7.4 collective-permute-start.1
  569.9 6.7 collective-permute-start.1
  577.4 7.4 collective-permute-start.1
  585.7 6.7 collective-permute-start.1
  593.3 7.4 collective-permute-start.1
  601.6 6.6 collective-permute-start.1
  609.1 7.4 collective-permute-start.1
  617.4 6.8 collective-permute-start.1
  625.1 6.8 collective-permute-start.1
  632.8 6.8 collective-permute-start.1
  640.4 6.8 collective-permute-start.1
  648.1 6.8 collective-permute-start.1
  655.8 6.8 collective-permute-start.1
  663.5 6.8 collective-permute-start.1
  786.1 145.3 %all-gather.8.cloned.1.call-start = ((), (), s32[]{:S(2)}) async-start(), calls=%async_computation.6 | async-start | bytes 1114112 | tf_op jit(solution)/shard_map/all_gather | solution.py:259
  (52 other events, 2124.5 us)
Sparse Core Ops, SparseCore 0:
  12.4 50.9 all-gather.3
  70.0 77.3 reduce-scatter.2
  150.3 46.9 all-gather.5
  786.3 95.2 reduce-scatter.4
  884.5 46.9 all-gather.7
where the time goes:
time: 948 us; the launch traced here: 941 us
  waiting for transfers between devices  404 us (43%)
  other arithmetic  188 us (20%)
  matrix products  150 us (16%)
  starting transfers between devices  86.5 us (9%)
  local copies, waits for them, and re-layouts  78.9 us (8%)
  loops' own time  17.5 us (2%)
  between operations  16.5 us (2%)
    ppermute x30, waiting for transfers between devices, from_behind(): return lax.ppermute(array, axis, pairs)  96.8 us
    reduce_scatter x1, waiting for transfers between devices, shards(): lax.psum_scatter((main_part + jnp.dot(grad_gates, gate_pair.T, preferred_...  95.3 us
    ppermute x30, starting transfers between devices, from_behind(): return lax.ppermute(array, axis, pairs)  86.3 us
    another operation x44, other arithmetic, block_step(): lax.linalg.triangular_solve(system, target, left_side=True, lower=True, u...  85.4 us
    reduce_scatter x1, waiting for transfers between devices, shards(): lax.psum_scatter(jnp.dot(scaled, down_weight, preferred_element_type=jnp....  75.9 us
    all_gather x1, waiting for transfers between devices, shards(): embedded = lax.all_gather(columns, 'inner', axis=1, tiled=True)  50.5 us
    all_gather x1, waiting for transfers between devices, shards(): lax.all_gather(grad_mixed, 'inner', axis=0, tiled=True)  47.1 us
    all_gather x1, waiting for transfers between devices, shards(): lax.all_gather(normed_float.astype(jnp.bfloat16), 'inner', axis=0, tiled=...  38.1 us
  transfers between devices with their start and end apart: 35, of which 35 were waited for; matrix products, arithmetic and copies ran while one was open for 1% of the time, Pallas kernels for 0%

commit v1 on v0

v1 whole, which is shorter than its diff:
```python
import functools

import jax
import jax.numpy as jnp
from jax import lax
from jax.experimental import pallas as pl
from jax.experimental.pallas import tpu as pltpu
from jax.sharding import PartitionSpec as P

STEPS = 32
EPS = 1e-06
F32 = jnp.float32
BF16 = jnp.bfloat16
MESH = pl.DeviceIdType.MESH
HIGHEST = lax.Precision.HIGHEST
NN = (((1,), (0,)), ((), ()))
NT = (((1,), (1,)), ((), ()))
TN = (((0,), (0,)), ((), ()))


def exact(left, right, dims=NN):
    return lax.dot_general(left, right, dims, precision=HIGHEST, preferred_element_type=F32)


def fast(left, right, dims=NN):
    return lax.dot_general(
        left.astype(BF16), right.astype(BF16), dims, preferred_element_type=F32
    )


def row_sum(values):
    return jnp.sum(values, axis=1, keepdims=True)


def unit_inverse(lower, rows, cols):
    size = lower.shape[0]
    eye = (rows == cols).astype(F32)
    inverse, span = eye, 1
    while span < size:
        joined = (rows // (2 * span) == cols // (2 * span)) & (rows // span != cols // span)
        below = jnp.where(joined, lower, 0.0)
        if span == 1:
            inverse = eye - below
        else:
            inverse = inverse - exact(inverse, exact(below, inverse))
        span *= 2
    return inverse


def delta_prepare(query_pre, key_pre, values, decay_pre, beta_pre, cot, rate, decay_bias, beta_bias):
    size, key_dim = key_pre.shape
    query_inv = lax.rsqrt(row_sum(query_pre * query_pre) + EPS)
    key_inv = lax.rsqrt(row_sum(key_pre * key_pre) + EPS)
    queries = query_pre * (query_inv * key_dim ** (-0.5))
    keys = key_pre * key_inv
    shifted = decay_pre + decay_bias
    soft = jnp.maximum(shifted, 0.0) + jnp.log1p(jnp.exp(-jnp.abs(shifted)))
    log_decay = -jnp.exp(rate) * soft
    betas = 1.0 / (1.0 + jnp.exp(-(beta_pre + beta_bias)))

    rows = lax.broadcasted_iota(jnp.int32, (size, size), 0)
    cols = lax.broadcasted_iota(jnp.int32, (size, size), 1)
    lower = rows >= cols
    ones_lower = lower.astype(F32)
    cum_rows = exact(ones_lower, jnp.broadcast_to(log_decay, (size, size)))
    cum_cols = cum_rows.T
    ratio = jnp.where(lower, jnp.exp(jnp.where(lower, cum_rows - cum_cols, 0.0)), 0.0)
    cum = cum_rows[:, 0:1]
    cum_last = cum_cols[:, size - 1 : size]
    grown = jnp.exp(cum)
    left_over = jnp.exp(cum_last - cum)
    total = jnp.exp(cum_last[0:1, :])

    key_gram = exact(keys, keys, NT)
    ratio_gram = jnp.where(rows > cols, ratio * key_gram, 0.0)
    strict = betas * ratio_gram
    inverse = unit_inverse(strict, rows, cols)
    scores = ratio * exact(queries, keys, NT)
    keys_grown = grown * keys
    queries_grown = grown * queries
    keys_tail = left_over * keys

    fresh_free = exact(inverse, betas * values)
    fresh_map = exact(inverse, betas * keys_grown)
    back_free = exact(inverse, exact(scores, cot, TN), TN)
    back_map = exact(inverse, keys_tail, TN)
    eye = (
        lax.broadcasted_iota(jnp.int32, (key_dim, key_dim), 0)
        == lax.broadcasted_iota(jnp.int32, (key_dim, key_dim), 1)
    ).astype(F32)
    transition = total * eye - exact(keys_tail, fresh_map, TN)
    transition_back = total * eye - exact(fresh_map, keys_tail, TN)
    offset = exact(keys_tail, fresh_free, TN)
    offset_back = exact(queries_grown, cot, TN) - exact(betas * keys_grown, back_free, TN)
    kept = dict(
        query_pre=query_pre, key_pre=key_pre, values=values, query_inv=query_inv, key_inv=key_inv,
        queries=queries, keys=keys, shifted=shifted, betas=betas, ratio=ratio, grown=grown,
        left_over=left_over, total=total, ratio_gram=ratio_gram, strict=strict, scores=scores,
        keys_grown=keys_grown, keys_tail=keys_tail, fresh_free=fresh_free, fresh_map=fresh_map,
        back_free=back_free, back_map=back_map, cot=cot, rate=rate,
    )
    return kept, (transition, offset), (transition_back, offset_back)


def delta_finish(kept, state, end_grad):
    k = kept
    size, key_dim = k["keys"].shape
    scale = key_dim ** (-0.5)
    rows = lax.broadcasted_iota(jnp.int32, (size, size), 0)
    cols = lax.broadcasted_iota(jnp.int32, (size, size), 1)
    fresh = k["fresh_free"] - exact(k["fresh_map"], state)
    back = k["back_free"] + exact(k["back_map"], end_grad)
    d_strict = jnp.where(rows > cols, -exact(back, fresh, NT), 0.0)
    d_gram = d_strict * (k["betas"] * k["ratio"])
    d_scores = exact(k["cot"], fresh, NT) * k["ratio"]
    residual = k["values"] - exact(k["keys_grown"], state)
    d_values = k["betas"] * back
    d_betas = row_sum(back * residual) + row_sum(d_strict * k["ratio_gram"])
    cot_state = k["grown"] * exact(k["cot"], state, NT)
    back_state = (k["grown"] * k["betas"]) * exact(back, state, NT)
    fresh_end = k["left_over"] * exact(fresh, end_grad, NT)
    d_queries = exact(d_scores, k["keys"]) + cot_state
    d_keys_read = exact(d_gram, k["keys"]) - back_state
    d_keys_write = exact(d_gram, k["keys"], TN) + exact(d_scores, k["queries"], TN) + fresh_end
    d_cum = row_sum(k["queries"] * d_queries) + row_sum(k["keys"] * (d_keys_read - d_keys_write))
    ends = jnp.sum(row_sum(k["keys"] * fresh_end), axis=0, keepdims=True) + k["total"] * jnp.sum(
        row_sum(state * end_grad), axis=0, keepdims=True
    )
    upper = (rows <= cols).astype(F32)
    d_log = exact(upper, jnp.broadcast_to(d_cum, (size, key_dim)))[:, 0:1] + ends

    query_inv, key_inv = k["query_inv"], k["key_inv"]
    d_query = (scale * query_inv) * (
        d_queries - k["query_pre"] * (query_inv * query_inv * row_sum(k["query_pre"] * d_queries))
    )
    d_keys = d_keys_read + d_keys_write
    d_key = key_inv * (d_keys - k["keys"] * row_sum(k["keys"] * d_keys))
    d_decay = d_log * (-jnp.exp(k["rate"])) * (1.0 / (1.0 + jnp.exp(-k["shifted"])))
    d_beta = d_betas * k["betas"] * (1.0 - k["betas"])
    return d_query, d_key, d_values, d_decay, d_beta


def kernel(
    chips, turn_of,
    columns_ref, step_ref, rate_ref, decay_bias_ref, beta_bias_ref, gain_one_ref, gain_two_ref,
    decay_ref, beta_ref, gate_hbm, up_hbm, down_hbm, query_hbm, key_hbm, value_hbm, cot_hbm,
    out_ref,
    gate_w, up_w, down_w, main_w, cot_v, gates_w, emb, normed, hidden, part, heap_one, heap_two,
    normed_two, grad_mixed, mixed_own, state_own, pair_map_out, pair_map_in, pair_off_out,
    pair_off_in, carry_in, carry_out, share_out, share_in,
    load_sem, send_sem, recv_sem, side_send, side_recv,
):
    me = lax.axis_index("inner")
    outer = lax.axis_index("outer")
    peers = lax.axis_size("inner")
    chip, core = outer // 2, lax.rem(outer, 2)
    partner = {"outer": outer + 1 - 2 * core}
    ahead = {"outer": lax.rem(chip + 1, chips) * 2 + core}
    behind = {"outer": lax.rem(chip + chips - 1, chips) * 2 + core}
    turn = chip + core * (chips - 1 - 2 * chip)
    onward = {"outer": lax.rem(chip + chips + 1 - 2 * core, chips) * 2 + core}

    key_dim = query_hbm.shape[1]
    value_dim = value_hbm.shape[1]
    width = down_hbm.shape[1]
    rows = columns_ref.shape[0]
    share = rows // peers
    slab = columns_ref.shape[1]

    loads = [
        pltpu.make_async_copy(gate_hbm, gate_w, load_sem.at[0]),
        pltpu.make_async_copy(up_hbm, up_w, load_sem.at[1]),
        pltpu.make_async_copy(down_hbm, down_w, load_sem.at[2]),
        pltpu.make_async_copy(query_hbm, main_w.at[:, pl.ds(0, key_dim)], load_sem.at[3]),
        pltpu.make_async_copy(key_hbm, main_w.at[:, pl.ds(key_dim, key_dim)], load_sem.at[4]),
        pltpu.make_async_copy(value_hbm, main_w.at[:, pl.ds(2 * key_dim, value_dim)], load_sem.at[5]),
        pltpu.make_async_copy(cot_hbm, cot_v, load_sem.at[6]),
    ]
    own_cols = pl.ds(pl.multiple_of(me * slab, slab), slab)
    own_rows = pl.ds(pl.multiple_of(me * share, share), share)
    place = pltpu.make_async_copy(columns_ref, emb.at[:, own_cols], load_sem.at[7])
    place.start()
    for load in loads:
        load.start()

    barrier = pltpu.get_barrier_semaphore()
    for step in range(1, peers):
        pl.semaphore_signal(
            barrier, inc=1, device_id={"inner": lax.rem(me + step, peers)}, device_id_type=MESH
        )
    for side in (partner, ahead, behind):
        pl.semaphore_signal(barrier, inc=1, device_id=side, device_id_type=MESH)
    pl.semaphore_wait(barrier, peers + 2)

    def to_peers(stage, source, target):
        copies = []
        for step in range(1, peers):
            peer = lax.rem(me + step, peers)
            copy = pltpu.make_async_remote_copy(
                src_ref=source(peer),
                dst_ref=target(step),
                send_sem=send_sem.at[stage, step - 1],
                recv_sem=recv_sem.at[stage, step - 1],
                device_id={"inner": peer},
                device_id_type=MESH,
            )
            copy.start()
            copies.append(copy)
        return copies

    def rows_of(owner):
        return pl.ds(pl.multiple_of(owner * share, share), share)

    copies = to_peers(0, lambda peer: columns_ref, lambda step: emb.at[:, own_cols])
    row_id = lax.broadcasted_iota(jnp.int32, (8, width), 0)
    gates_w[...] = jnp.where(
        row_id == 0,
        decay_ref[...].astype(F32),
        jnp.where(row_id == 1, beta_ref[...].astype(F32), 0.0),
    )
    place.wait()
    for copy in copies:
        copy.wait()

    def norm_one(index, carry):
        at = pl.ds(pl.multiple_of(index * 16, 16), 16)
        values = emb[at, :].astype(F32)
        scale = lax.rsqrt(row_sum(values * values) * (1.0 / width) + EPS)
        normed[at, :] = (values * scale * gain_one_ref[...]).astype(BF16)
        return carry

    lax.fori_loop(0, rows // 16, norm_one, 0)
    loads[0].wait()
    loads[1].wait()
    gate_rows = jnp.dot(normed[...], gate_w[...], preferred_element_type=F32)
    up_rows = jnp.dot(normed[...], up_w[...], preferred_element_type=F32)
    active = gate_rows * (1.0 / (1.0 + jnp.exp(-gate_rows))) * up_rows
    hidden[...] = active
    path_scale = (step_ref[...].astype(F32) + 0.5) / STEPS
    scaled = (path_scale * active).astype(BF16)
    loads[2].wait()
    for piece in range(width // 256):
        at = slice(piece * 256, piece * 256 + 256)
        part[:, at] = jnp.dot(scaled, down_w[:, at], preferred_element_type=F32).astype(BF16)

    def reduce_rows(stage, heap):
        copies = to_peers(stage, lambda peer: part.at[rows_of(peer), :], lambda step: heap.at[step - 1])
        acc = part[own_rows, :].astype(F32)
        for step, copy in enumerate(copies):
            copy.wait()
            acc = acc + heap[step].astype(F32)
        return acc

    mixed = emb[own_rows, :].astype(F32) + reduce_rows(1, heap_one)
    mixed_own[...] = mixed
    inv_two = lax.rsqrt(row_sum(mixed * mixed) * (1.0 / width) + EPS)
    normed_two[own_rows, :] = (mixed * inv_two * gain_two_ref[...]).astype(BF16)

    def spread_rows(stage, array):
        copies = to_peers(stage, lambda peer: array.at[own_rows, :], lambda step: array.at[own_rows, :])
        for copy in copies:
            copy.wait()

    spread_rows(2, normed_two)
    for load in loads[3:]:
        load.wait()
    main = jnp.dot(normed_two[...], main_w[...], preferred_element_type=F32)
    gates = lax.dot_general(
        normed_two[...], gates_w[...].astype(BF16), NT, preferred_element_type=F32
    )
    kept, ahead_map, back_map = delta_prepare(
        main[:, :key_dim],
        main[:, key_dim : 2 * key_dim],
        main[:, 2 * key_dim :],
        gates[:, 0:1],
        gates[:, 1:2],
        cot_v[...].astype(F32),
        rate_ref[...],
        decay_bias_ref[...],
        beta_bias_ref[...],
    )

    first = core == 0
    own_map = jnp.where(first, ahead_map[0], back_map[0])
    own_off = jnp.where(first, ahead_map[1], back_map[1])
    pair_map_out[...] = jnp.where(first, back_map[0], ahead_map[0])
    pair_off_out[...] = jnp.where(first, back_map[1], ahead_map[1]).astype(BF16)

    def to_side(index, source, target, device):
        return pltpu.make_async_remote_copy(
            src_ref=source,
            dst_ref=target,
            send_sem=side_send.at[index],
            recv_sem=side_recv.at[index],
            device_id=device,
            device_id_type=MESH,
        )

    pair_copies = [
        to_side(0, pair_map_out, pair_map_in, partner),
        to_side(1, pair_off_out, pair_off_in, partner),
    ]
    for copy in pair_copies:
        copy.start()
    for copy in pair_copies:
        copy.wait()
    chip_map = exact(pair_map_in[...], own_map)
    chip_off = exact(pair_map_in[...], own_off) + pair_off_in[...].astype(F32)

    pass_on = to_side(2, carry_out, carry_in, onward)

    @pl.when(turn == 0)
    def _():
        carry_in[...] = jnp.zeros_like(carry_in)

    @pl.when(turn > 0)
    def _():
        pass_on.wait_recv()

    @pl.when(turn < chips - 1)
    def _():
        carry_out[...] = (exact(chip_map, carry_in[...].astype(F32)) + chip_off).astype(BF16)
        pass_on.start()

    carried = carry_in[...].astype(F32)
    share_out[...] = (exact(own_map, carried) + own_off).astype(BF16)
    swap = to_side(3, share_out, share_in, partner)
    swap.start()
    swap.wait()
    other = share_in[...].astype(F32)
    state = jnp.where(first, carried, other)
    end_grad = jnp.where(first, other, carried)
    d_query, d_key, d_value, d_decay, d_beta = delta_finish(kept, state, end_grad)

    @pl.when(turn < chips - 1)
    def _():
        pass_on.wait_send()

    grads = jnp.concatenate([d_query, d_key, d_value], axis=1).astype(BF16)
    d_decay = d_decay.astype(BF16).astype(F32)
    d_beta = d_beta.astype(BF16).astype(F32)
    for piece in range(width // 256):
        at = slice(piece * 256, piece * 256 + 256)
        back = lax.dot_general(grads, main_w[at, :], NT, preferred_element_type=F32)
        back = back + d_decay * gates_w[0:1, at] + d_beta * gates_w[1:2, at]
        part[:, at] = back.astype(BF16)
    back = reduce_rows(3, heap_two)
    mixed = mixed_own[...]
    inv_two = lax.rsqrt(row_sum(mixed * mixed) * (1.0 / width) + EPS)
    gained = back * gain_two_ref[...]
    inner_sum = row_sum(mixed * gained) * (1.0 / width)
    grad_mixed[own_rows, :] = (
        inv_two * gained - mixed * (inv_two * inv_two * inv_two * inner_sum)
    ).astype(BF16)
    spread_rows(4, grad_mixed)
    out_ref[...] = hidden[...] * lax.dot_general(
        grad_mixed[...], down_w[...], NT, preferred_element_type=F32
    )


def shards(
    tokens, step_index, embed_table, gain_one, gate_weight, up_weight, down_weight, gain_two,
    query_weight, key_weight, value_weight, decay_weight, beta_weight, rate_log, decay_bias,
    beta_bias, cotangent,
):
    columns = embed_table.at[tokens].get(mode="promise_in_bounds")
    peers = lax.axis_size("inner")
    chips = lax.axis_size("outer") // 2
    rows, slab = columns.shape
    width = slab * peers
    hidden_dim = gate_weight.shape[1]
    key_dim, value_dim = query_weight.shape[1], value_weight.shape[1]
    share = rows // peers
    in_vmem = pl.BlockSpec(memory_space=pltpu.VMEM)
    in_place = pl.BlockSpec(memory_space=pl.ANY)
    vm = pltpu.VMEM
    return pl.pallas_call(
        functools.partial(kernel, chips, None),
        out_shape=jax.ShapeDtypeStruct((rows, hidden_dim), F32),
        in_specs=[in_vmem] * 9 + [in_place] * 7,
        out_specs=in_vmem,
        scratch_shapes=[
            vm((width, hidden_dim), BF16),
            vm((width, hidden_dim), BF16),
            vm((hidden_dim, width), BF16),
            vm((width, 2 * key_dim + value_dim), BF16),
            vm((rows, value_dim), BF16),
            vm((8, width), F32),
            vm((rows, width), BF16),
            vm((rows, width), BF16),
            vm((rows, hidden_dim), F32),
            vm((rows, width), BF16),
            vm((peers - 1, share, width), BF16),
            vm((peers - 1, share, width), BF16),
            vm((rows, width), BF16),
            vm((rows, width), BF16),
            vm((share, width), F32),
            vm((key_dim, value_dim), F32),
            vm((key_dim, key_dim), F32),
            vm((key_dim, key_dim), F32),
            vm((key_dim, value_dim), BF16),
            vm((key_dim, value_dim), BF16),
            vm((key_dim, value_dim), BF16),
            vm((key_dim, value_dim), BF16),
            vm((key_dim, value_dim), BF16),
            vm((key_dim, value_dim), BF16),
            pltpu.SemaphoreType.DMA((8,)),
            pltpu.SemaphoreType.DMA((5, peers - 1)),
            pltpu.SemaphoreType.DMA((5, peers - 1)),
            pltpu.SemaphoreType.DMA((4,)),
            pltpu.SemaphoreType.DMA((4,)),
        ],
        compiler_params=pltpu.CompilerParams(collective_id=0, has_side_effects=True),
        name="attribution",
    )(
        columns,
        step_index.reshape(1, 1),
        rate_log.reshape(1, 1),
        decay_bias.reshape(1, 1),
        beta_bias.reshape(1, 1),
        gain_one.reshape(1, width),
        gain_two.reshape(1, width),
        decay_weight.reshape(1, width),
        beta_weight.reshape(1, width),
        gate_weight,
        up_weight,
        down_weight,
        query_weight,
        key_weight,
        value_weight,
        cotangent,
    )


def solution(mesh):
    placed = (
        P("outer"), P(), P(None, "inner"), P(), P(None, "inner"), P(None, "inner"),
        P("inner", None), P(), P(None, "inner"), P(None, "inner"), P(None, "inner"),
        P(None, "inner"), P(None, "inner"), P("inner"), P("inner"), P("inner"),
        P("outer", "inner"),
    )
    return jax.shard_map(
        shards, mesh=mesh, in_specs=placed, out_specs=P("outer", "inner"), check_vma=False
    )
```

time: 948 us -> 144 us (0.15)
  the two profiles are of different devices: /device:TPU:2 before, /device:TPU:232 now
where the time goes in v1:
time: 144 us
  Pallas kernels  130 us (90%)
  local copies, waits for them, and re-layouts  10.2 us (7%)
  between operations  2.6 us (2%)
    pallas_call x1, Pallas kernels, shards(): pl.pallas_call(functools.partial(kernel, chips, None), out_shape=jax.Shap...  130 us
    unnamed x4, local copies, waits for them, and re-layouts  4.26 us
    gather x1, local copies, waits for them, and re-layouts, shards(): columns = embed_table.at[tokens].get(mode='promise_in_bounds')  4.07 us

profile of v1, /device:TPU:232, one launch (start us, length us, event | category | flops | bytes accessed | tf_op | source)
XLA Modules:
  0.0 143.6 jit_solution(15959569404636118025)
XLA Ops:
  2.6 0.7 compare_select_fusion
  3.3 4.1 %gather_fusion = bf16[256,128]{1,0:T(8,128)(2,1)} fusion(bf16[16384,128]{1,0:T(8,128)(2,1)} %param.19, s32[1024]{0:T(1024)S(1)} %pad_clamp_fusion), kind=kCustom, calls=%fused_computation | custom fusion | bytes 132096 | tf_op jit(solution)/shard_map/gather | solution.py:366
  7.3 0.0 copy-start
  7.4 2.7 %copy.18.gate_hbm = bf16[2048,352]{1,0:T(8,128)(2,1)} copy(bf16[2048,352]{0,1:T(8,128)(2,1)} %param.21) | data formatting | bytes 2883584 | tf_op args[4]
  10.0 0.0 copy-done
  10.0 1.6 %copy.19.up_hbm = bf16[2048,352]{1,0:T(8,128)(2,1)} copy(bf16[2048,352]{0,1:T(8,128)(2,1)S(1)} %copy-done) | data formatting | bytes 2883584 | tf_op args[5]
  11.6 130.0 %attribution.1 = f32[256,352]{1,0:T(8,128)} custom-call(bf16[256,128]{1,0:T(8,128)(2,1)} %gather_fusion, s32[1,1]{1,0:T(1,128)} %bitcast.8.step_ref, f32[1,1]{1,0:T(1,128)} %bitcast.9.rate_ref, f32[1,1]{1,0:T(1,128)} %bitcast.10.decay_bias_ref, f32[1,1]{1,0:T(1,128)} %bitcast.11.beta_bias_ref, f32[1,2048]{1,0:T(1,128)} %bitcast.12, f32[1,2048]{1,0:T(1,128)} %bitcast.13, ...), custom_call_target="tpu_custom_call" | custom-call | tf_op jit(solution)/shard_map/attribution/pallas_call | solution.py:377
  141.7 1.9 %copy.20 = f32[256,352]{0,1:T(8,128)} copy(f32[256,352]{1,0:T(8,128)} %attribution.1) | data formatting | bytes 720896 | tf_op jit(solution)/shard_map/attribution/pallas_call | solution.py:377
  (1 shorter events, 0.0 us)
Async XLA Ops:
  7.3 2.7 %copy-start = (bf16[2048,352]{0,1:T(8,128)(2,1)S(1)}, bf16[2048,352]{0,1:T(8,128)(2,1)}, u32[]{:S(2)}) copy-start(bf16[2048,352]{0,1:T(8,128)(2,1)} %param.22) | copy-start | bytes 4325380

commit v2 on v1

v2 whole, which is shorter than its diff:
```python
import functools

import jax
import jax.numpy as jnp
from jax import lax
from jax.experimental import pallas as pl
from jax.experimental.pallas import tpu as pltpu
from jax.sharding import PartitionSpec as P

STEPS = 32
EPS = 1e-06
F32 = jnp.float32
BF16 = jnp.bfloat16
MESH = pl.DeviceIdType.MESH
HIGHEST = lax.Precision.HIGHEST
NN = (((1,), (0,)), ((), ()))
NT = (((1,), (1,)), ((), ()))
TN = (((0,), (0,)), ((), ()))


def exact(left, right, dims=NN):
    return lax.dot_general(left, right, dims, precision=HIGHEST, preferred_element_type=F32)


def fast(left, right, dims=NN):
    return lax.dot_general(
        left.astype(BF16), right.astype(BF16), dims, preferred_element_type=F32
    )


def row_sum(values):
    return jnp.sum(values, axis=1, keepdims=True)


def split(value):
    high = value.astype(BF16)
    return high, (value - high.astype(F32)).astype(BF16)


def triple(left, right, dims=NN):
    left_high, left_low = split(left)
    right_high, right_low = split(right)

    def dot(one, two):
        return lax.dot_general(one, two, dims, preferred_element_type=F32)

    return dot(left_high, right_high) + (dot(left_high, right_low) + dot(left_low, right_high))


near = triple
solve = triple
gram = triple


def unit_inverse(lower, rows, cols):
    size = lower.shape[0]
    eye = (rows == cols).astype(F32)
    inverse, span = eye, 1
    while span < size:
        joined = (rows // (2 * span) == cols // (2 * span)) & (rows // span != cols // span)
        below = jnp.where(joined, lower, 0.0)
        if span == 1:
            inverse = eye - below
        else:
            inverse = inverse - solve(inverse, solve(below, inverse))
        span *= 2
    return inverse


def delta_prepare(query_pre, key_pre, values, decay_pre, beta_pre, cot, rate, decay_bias, beta_bias):
    size, key_dim = key_pre.shape
    query_inv = lax.rsqrt(row_sum(query_pre * query_pre) + EPS)
    key_inv = lax.rsqrt(row_sum(key_pre * key_pre) + EPS)
    queries = query_pre * (query_inv * key_dim ** (-0.5))
    keys = key_pre * key_inv
    shifted = decay_pre + decay_bias
    soft = jnp.maximum(shifted, 0.0) + jnp.log1p(jnp.exp(-jnp.abs(shifted)))
    log_decay = -jnp.exp(rate) * soft
    betas = 1.0 / (1.0 + jnp.exp(-(beta_pre + beta_bias)))

    rows = lax.broadcasted_iota(jnp.int32, (size, size), 0)
    cols = lax.broadcasted_iota(jnp.int32, (size, size), 1)
    lower = rows >= cols
    ones_lower = lower.astype(F32)
    cum_rows = exact(ones_lower, jnp.broadcast_to(log_decay, (size, size)))
    cum_cols = cum_rows.T
    ratio = jnp.where(lower, jnp.exp(jnp.where(lower, cum_rows - cum_cols, 0.0)), 0.0)
    cum = cum_rows[:, 0:1]
    cum_last = cum_cols[:, size - 1 : size]
    grown = jnp.exp(cum)
    left_over = jnp.exp(cum_last - cum)
    total = jnp.exp(cum_last[0:1, :])

    key_gram = gram(keys, keys, NT)
    ratio_gram = jnp.where(rows > cols, ratio * key_gram, 0.0)
    strict = betas * ratio_gram
    inverse = unit_inverse(strict, rows, cols)
    scores = ratio * near(queries, keys, NT)
    keys_grown = grown * keys
    queries_grown = grown * queries
    keys_tail = left_over * keys

    fresh_free = near(inverse, betas * values)
    fresh_map = near(inverse, betas * keys_grown)
    back_free = near(inverse, near(scores, cot, TN), TN)
    back_map = near(inverse, keys_tail, TN)
    eye = (
        lax.broadcasted_iota(jnp.int32, (key_dim, key_dim), 0)
        == lax.broadcasted_iota(jnp.int32, (key_dim, key_dim), 1)
    ).astype(F32)
    transition = total * eye - near(keys_tail, fresh_map, TN)
    transition_back = total * eye - near(fresh_map, keys_tail, TN)
    offset = near(keys_tail, fresh_free, TN)
    offset_back = near(queries_grown, cot, TN) - near(betas * keys_grown, back_free, TN)
    kept = dict(
        query_pre=query_pre, key_pre=key_pre, values=values, query_inv=query_inv, key_inv=key_inv,
        queries=queries, keys=keys, shifted=shifted, betas=betas, ratio=ratio, grown=grown,
        left_over=left_over, total=total, ratio_gram=ratio_gram, strict=strict, scores=scores,
        keys_grown=keys_grown, keys_tail=keys_tail, fresh_free=fresh_free, fresh_map=fresh_map,
        back_free=back_free, back_map=back_map, cot=cot, rate=rate,
    )
    return kept, (transition, offset), (transition_back, offset_back)


def delta_finish(kept, state, end_grad):
    k = kept
    size, key_dim = k["keys"].shape
    scale = key_dim ** (-0.5)
    rows = lax.broadcasted_iota(jnp.int32, (size, size), 0)
    cols = lax.broadcasted_iota(jnp.int32, (size, size), 1)
    fresh = k["fresh_free"] - near(k["fresh_map"], state)
    back = k["back_free"] + near(k["back_map"], end_grad)
    d_strict = jnp.where(rows > cols, -near(back, fresh, NT), 0.0)
    d_gram = d_strict * (k["betas"] * k["ratio"])
    d_scores = near(k["cot"], fresh, NT) * k["ratio"]
    residual = k["values"] - near(k["keys_grown"], state)
    d_values = k["betas"] * back
    d_betas = row_sum(back * residual) + row_sum(d_strict * k["ratio_gram"])
    cot_state = k["grown"] * near(k["cot"], state, NT)
    back_state = (k["grown"] * k["betas"]) * near(back, state, NT)
    fresh_end = k["left_over"] * near(fresh, end_grad, NT)
    d_queries = near(d_scores, k["keys"]) + cot_state
    d_keys_read = near(d_gram, k["keys"]) - back_state
    d_keys_write = near(d_gram, k["keys"], TN) + near(d_scores, k["queries"], TN) + fresh_end
    d_cum = row_sum(k["queries"] * d_queries) + row_sum(k["keys"] * (d_keys_read - d_keys_write))
    ends = jnp.sum(row_sum(k["keys"] * fresh_end), axis=0, keepdims=True) + k["total"] * jnp.sum(
        row_sum(state * end_grad), axis=0, keepdims=True
    )
    upper = (rows <= cols).astype(F32)
    d_log = exact(upper, jnp.broadcast_to(d_cum, (size, key_dim)))[:, 0:1] + ends

    query_inv, key_inv = k["query_inv"], k["key_inv"]
    d_query = (scale * query_inv) * (
        d_queries - k["query_pre"] * (query_inv * query_inv * row_sum(k["query_pre"] * d_queries))
    )
    d_keys = d_keys_read + d_keys_write
    d_key = key_inv * (d_keys - k["keys"] * row_sum(k["keys"] * d_keys))
    d_decay = d_log * (-jnp.exp(k["rate"])) * (1.0 / (1.0 + jnp.exp(-k["shifted"])))
    d_beta = d_betas * k["betas"] * (1.0 - k["betas"])
    return d_query, d_key, d_values, d_decay, d_beta


def ring_order(side):
    return sorted(range(1, side), key=lambda step: (-min(step, side - step), step))


def kernel(
    chips,
    tokens_ref, step_ref, rate_ref, decay_bias_ref, beta_bias_ref, gain_one_ref, gain_two_ref,
    decay_ref, beta_ref, table_hbm, gate_hbm, up_hbm, down_hbm, query_hbm, key_hbm, value_hbm,
    cot_hbm,
    out_ref,
    table, gate_w, up_w, down_w, main_w, cot_v, gates_w, emb, normed, hidden, part,
    heap_one, heap_two, sums, last_one, last_two,
    normed_two, grad_mixed, mixed_own, pair_map_out, pair_map_in, pair_off_out,
    pair_off_in, carry_in, carry_out, share_out, share_in,
    load_sem, send_sem, recv_sem, side_send, side_recv,
):
    me = lax.axis_index("inner")
    outer = lax.axis_index("outer")
    peers = lax.axis_size("inner")
    side = int(round(peers**0.5))
    line, spot = me // side, lax.rem(me, side)
    chip, core = outer // 2, lax.rem(outer, 2)
    partner = {"outer": outer + 1 - 2 * core}
    ahead = {"outer": lax.rem(chip + 1, chips) * 2 + core}
    behind = {"outer": lax.rem(chip + chips - 1, chips) * 2 + core}
    turn = chip + core * (chips - 1 - 2 * chip)
    onward = {"outer": lax.rem(chip + chips + 1 - 2 * core, chips) * 2 + core}

    key_dim = query_hbm.shape[1]
    value_dim = value_hbm.shape[1]
    width = down_hbm.shape[1]
    half = width // 2
    rows = tokens_ref.shape[0]
    share = rows // peers
    slab = table.shape[2]

    loads = [
        pltpu.make_async_copy(gate_hbm, gate_w, load_sem.at[0]),
        pltpu.make_async_copy(up_hbm, up_w, load_sem.at[1]),
        pltpu.make_async_copy(down_hbm, down_w, load_sem.at[2]),
        pltpu.make_async_copy(query_hbm, main_w.at[:, pl.ds(0, key_dim)], load_sem.at[3]),
        pltpu.make_async_copy(key_hbm, main_w.at[:, pl.ds(key_dim, key_dim)], load_sem.at[4]),
        pltpu.make_async_copy(value_hbm, main_w.at[:, pl.ds(2 * key_dim, value_dim)], load_sem.at[5]),
        pltpu.make_async_copy(cot_hbm, cot_v, load_sem.at[6]),
    ]
    table_load = pltpu.make_async_copy(table_hbm, table, load_sem.at[7])
    table_load.start()

    barrier = pltpu.get_barrier_semaphore()
    for step in range(1, side):
        for peer in (
            lax.rem(line + step, side) * side + spot,
            line * side + lax.rem(spot + step, side),
        ):
            pl.semaphore_signal(barrier, inc=1, device_id={"inner": peer}, device_id_type=MESH)
    for device in (partner, ahead, behind):
        pl.semaphore_signal(barrier, inc=1, device_id=device, device_id_type=MESH)
    for load in loads:
        load.start()

    row_id = lax.broadcasted_iota(jnp.int32, (8, width), 0)
    gates_w[...] = jnp.where(
        row_id == 0,
        decay_ref[...].astype(F32),
        jnp.where(row_id == 1, beta_ref[...].astype(F32), 0.0),
    )

    table_load.wait()
    tile_row = lax.broadcasted_iota(jnp.int32, (8, slab), 0)

    def pick(index, carry):
        found = []
        for part_of in range(2):
            tile = jnp.zeros((8, slab), F32)
            for row in range(8):
                token = tokens_ref[index * 16 + part_of * 8 + row]
                near_rows = table[lax.shift_right_logical(token, 3)].astype(F32)
                chosen = jnp.sum(
                    jnp.where(tile_row == (token & 7), near_rows, 0.0), axis=0, keepdims=True
                )
                tile = jnp.where(tile_row == row, chosen, tile)
            found.append(tile)
        emb[me, pl.ds(pl.multiple_of(index * 16, 16), 16), :] = jnp.concatenate(
            found, axis=0
        ).astype(BF16)
        return carry

    lax.fori_loop(0, rows // 16, pick, 0)
    pl.semaphore_wait(barrier, 2 * (side - 1) + 3)

    def to_axis(across, step):
        if across:
            return line * side + lax.rem(spot + step, side)
        return lax.rem(line + step, side) * side + spot

    def send(stage, way, index, source, target, peer):
        copy = pltpu.make_async_remote_copy(
            src_ref=source,
            dst_ref=target,
            send_sem=send_sem.at[stage, way, index],
            recv_sem=recv_sem.at[stage, way, index],
            device_id={"inner": peer},
            device_id_type=MESH,
        )
        copy.start()
        return copy

    order = ring_order(side)

    def spread(stage, piece):
        first_hop, second_hop = [{}, {}], []
        for step in order:
            for way in range(2):
                own = piece(me, way)
                first_hop[way][step] = send(stage, way, step - 1, own, own, to_axis(way, step))
        for step in order:
            for way in range(2):
                own = piece(me, way)
                second_hop.append(
                    send(stage, way, side - 1 + step - 1, own, own, to_axis(1 - way, step))
                )
        for gone in reversed(order):
            for way in range(2):
                first_hop[way][gone].wait_recv()
                got = piece(to_axis(way, side - gone), way)
                for step in order:
                    index = (side - 1) * (1 + gone) + step - 1
                    second_hop.append(send(stage, way, index, got, got, to_axis(1 - way, step)))
        for copy in second_hop:
            copy.wait()
        for way in range(2):
            for step in order:
                first_hop[way][step].wait_send()

    def reduce_send(stage, heap, way):
        hops = {}
        for apart in order + [0]:
            for step in order:
                if way == 0:
                    at = (lax.rem(line + apart, side), lax.rem(spot + step, side))
                else:
                    at = (lax.rem(line + step, side), lax.rem(spot + apart, side))
                index = apart * (side - 1) + step - 1
                hops[apart, step] = send(
                    stage, way, index, part.at[way, at[0], at[1]], heap.at[way, index],
                    to_axis(1 - way, step),
                )
        return hops

    def reduce_finish(stage, heap, last, hops):
        own, second_hop = [None, None], [[], []]
        for apart in order + [0]:
            for way in range(2):
                if way == 0:
                    at = (lax.rem(line + apart, side), spot)
                else:
                    at = (line, lax.rem(spot + apart, side))
                total = part[way, at[0], at[1]].astype(F32)
                for step in reversed(order):
                    hops[way][apart, step].wait_recv()
                    total = total + heap[way, apart * (side - 1) + step - 1].astype(F32)
                if apart == 0:
                    own[way] = total
                else:
                    sums[way, apart - 1] = total.astype(BF16)
                    second_hop[way].append(
                        (apart, send(
                            stage, way, side * (side - 1) + apart - 1, sums.at[way, apart - 1],
                            last.at[way, apart - 1], to_axis(way, apart),
                        ))
                    )
        for way in range(2):
            for apart, copy in second_hop[way]:
                copy.wait()
                own[way] = own[way] + last[way, apart - 1].astype(F32)
            for copy in hops[way].values():
                copy.wait_send()
        return jnp.concatenate(own, axis=1)

    spread(0, lambda owner, way: emb.at[owner, pl.ds(way * (rows // 2), rows // 2), :])

    def norm_one(index, carry):
        at = pl.ds(pl.multiple_of(index * 16, 16), 16)
        values = [emb[owner, at, :].astype(F32) for owner in range(peers)]
        squares = values[0] * values[0]
        for value in values[1:]:
            squares = squares + value * value
        scale = lax.rsqrt(row_sum(squares) * (1.0 / width) + EPS)
        for owner, value in enumerate(values):
            cut = slice(owner * slab, (owner + 1) * slab)
            normed[at, cut] = (value * scale * gain_one_ref[:, cut]).astype(BF16)
        return carry

    lax.fori_loop(0, rows // 16, norm_one, 0, unroll=2)
    loads[0].wait()
    loads[1].wait()
    gate_rows = lax.dot_general(normed[...], gate_w[...], NT, preferred_element_type=F32)
    up_rows = lax.dot_general(normed[...], up_w[...], NT, preferred_element_type=F32)
    active = gate_rows * (1.0 / (1.0 + jnp.exp(-gate_rows))) * up_rows
    path_scale = (step_ref[...].astype(F32) + 0.5) / STEPS
    scaled = (path_scale * active).astype(BF16)
    loads[2].wait()

    def partial_half(way, product):
        for first in range(way * half, way * half + half, 256):
            block = product(slice(first, first + 256)).astype(BF16)
            at = slice(first - way * half, first - way * half + 256)
            part[way, :, :, :, at] = block.reshape(side, side, share, 256)

    hops = []
    for way in range(2):
        partial_half(
            way, lambda at: jnp.dot(scaled, down_w[:, at], preferred_element_type=F32)
        )
        hops.append(reduce_send(1, heap_one, way))
    hidden[...] = active.T
    own_rows = pl.ds(pl.multiple_of(me * share, share), share)
    own_emb = jnp.concatenate([emb[owner, own_rows, :] for owner in range(peers)], axis=1)
    mixed = own_emb.astype(F32) + reduce_finish(1, heap_one, last_one, hops)
    mixed_own[...] = mixed
    inv_two = lax.rsqrt(row_sum(mixed * mixed) * (1.0 / width) + EPS)
    normed_two[own_rows, :] = (mixed * inv_two * gain_two_ref[...]).astype(BF16)

    def row_piece(array):
        return lambda owner, way: array.at[
            pl.ds(pl.multiple_of(owner * share, share), share), pl.ds(way * half, half)
        ]

    spread(2, row_piece(normed_two))
    for load in loads[3:]:
        load.wait()
    main = jnp.dot(normed_two[...], main_w[...], preferred_element_type=F32)
    gates = lax.dot_general(
        normed_two[...], gates_w[...].astype(BF16), NT, preferred_element_type=F32
    )
    kept, ahead_map, back_map = delta_prepare(
        main[:, :key_dim],
        main[:, key_dim : 2 * key_dim],
        main[:, 2 * key_dim :],
        gates[:, 0:1],
        gates[:, 1:2],
        cot_v[...].astype(F32),
        rate_ref[...],
        decay_bias_ref[...],
        beta_bias_ref[...],
    )

    first = core == 0
    own_map = jnp.where(first, ahead_map[0], back_map[0])
    own_off = jnp.where(first, ahead_map[1], back_map[1])
    pair_map_out[...] = jnp.where(first, back_map[0], ahead_map[0])
    pair_off_out[...] = jnp.where(first, back_map[1], ahead_map[1]).astype(BF16)

    def to_side(index, source, target, device):
        return pltpu.make_async_remote_copy(
            src_ref=source,
            dst_ref=target,
            send_sem=side_send.at[index],
            recv_sem=side_recv.at[index],
            device_id=device,
            device_id_type=MESH,
        )

    pair_copies = [
        to_side(0, pair_map_out, pair_map_in, partner),
        to_side(1, pair_off_out, pair_off_in, partner),
    ]
    for copy in pair_copies:
        copy.start()
    for copy in pair_copies:
        copy.wait()
    chip_map = exact(pair_map_in[...], own_map)
    chip_off = exact(pair_map_in[...], own_off) + pair_off_in[...].astype(F32)

    pass_on = to_side(2, carry_out, carry_in, onward)

    @pl.when(turn == 0)
    def _():
        carry_in[...] = jnp.zeros_like(carry_in)

    @pl.when(turn > 0)
    def _():
        pass_on.wait_recv()

    @pl.when(turn < chips - 1)
    def _():
        carry_out[...] = (exact(chip_map, carry_in[...].astype(F32)) + chip_off).astype(BF16)
        pass_on.start()

    carried = carry_in[...].astype(F32)
    share_out[...] = (exact(own_map, carried) + own_off).astype(BF16)
    swap = to_side(3, share_out, share_in, partner)
    swap.start()
    swap.wait()
    other = share_in[...].astype(F32)
    state = jnp.where(first, carried, other)
    end_grad = jnp.where(first, other, carried)
    d_query, d_key, d_value, d_decay, d_beta = delta_finish(kept, state, end_grad)

    @pl.when(turn < chips - 1)
    def _():
        pass_on.wait_send()

    grads = jnp.concatenate([d_query, d_key, d_value], axis=1).astype(BF16)
    d_decay = d_decay.astype(BF16).astype(F32)
    d_beta = d_beta.astype(BF16).astype(F32)

    def back_block(at):
        block = lax.dot_general(grads, main_w[at, :], NT, preferred_element_type=F32)
        return block + d_decay * gates_w[0:1, at] + d_beta * gates_w[1:2, at]

    hops = []
    for way in range(2):
        partial_half(way, back_block)
        hops.append(reduce_send(3, heap_two, way))
    back = reduce_finish(3, heap_two, last_two, hops)
    mixed = mixed_own[...]
    inv_two = lax.rsqrt(row_sum(mixed * mixed) * (1.0 / width) + EPS)
    gained = back * gain_two_ref[...]
    inner_sum = row_sum(mixed * gained) * (1.0 / width)
    grad_mixed[own_rows, :] = (
        inv_two * gained - mixed * (inv_two * inv_two * inv_two * inner_sum)
    ).astype(BF16)
    spread(4, row_piece(grad_mixed))
    out_ref[...] = hidden[...] * lax.dot_general(
        down_w[...], grad_mixed[...], NT, preferred_element_type=F32
    )


def shards(
    tokens, step_index, embed_table, gain_one, gate_weight, up_weight, down_weight, gain_two,
    query_weight, key_weight, value_weight, decay_weight, beta_weight, rate_log, decay_bias,
    beta_bias, cotangent,
):
    peers = lax.axis_size("inner")
    side = int(round(peers**0.5))
    chips = lax.axis_size("outer") // 2
    rows = tokens.shape[0]
    words, slab = embed_table.shape
    width = slab * peers
    hidden_dim = gate_weight.shape[1]
    key_dim, value_dim = query_weight.shape[1], value_weight.shape[1]
    share = rows // peers
    in_vmem = pl.BlockSpec(memory_space=pltpu.VMEM)
    in_smem = pl.BlockSpec(memory_space=pltpu.SMEM)
    in_place = pl.BlockSpec(memory_space=pl.ANY)
    vm = pltpu.VMEM
    messages = (side + 1) * (side - 1)
    state = (key_dim, value_dim)
    attribution = pl.pallas_call(
        functools.partial(kernel, chips),
        out_shape=jax.ShapeDtypeStruct((hidden_dim, rows), F32),
        in_specs=[in_smem] + [in_vmem] * 8 + [in_place] * 8,
        out_specs=in_vmem,
        scratch_shapes=[
            vm((words // 8, 8, slab), BF16),
            vm((hidden_dim, width), BF16),
            vm((hidden_dim, width), BF16),
            vm((hidden_dim, width), BF16),
            vm((width, 2 * key_dim + value_dim), BF16),
            vm((rows, value_dim), BF16),
            vm((8, width), F32),
            vm((peers, rows, slab), BF16),
            vm((rows, width), BF16),
            vm((hidden_dim, rows), F32),
            vm((2, side, side, share, width // 2), BF16),
            vm((2, side * (side - 1), share, width // 2), BF16),
            vm((2, side * (side - 1), share, width // 2), BF16),
            vm((2, side - 1, share, width // 2), BF16),
            vm((2, side - 1, share, width // 2), BF16),
            vm((2, side - 1, share, width // 2), BF16),
            vm((rows, width), BF16),
            vm((rows, width), BF16),
            vm((share, width), F32),
            vm((key_dim, key_dim), F32),
            vm((key_dim, key_dim), F32),
            vm(state, BF16),
            vm(state, BF16),
            vm(state, BF16),
            vm(state, BF16),
            vm(state, BF16),
            vm(state, BF16),
            pltpu.SemaphoreType.DMA((8,)),
            pltpu.SemaphoreType.DMA((5, 2, messages)),
            pltpu.SemaphoreType.DMA((5, 2, messages)),
            pltpu.SemaphoreType.DMA((4,)),
            pltpu.SemaphoreType.DMA((4,)),
        ],
        compiler_params=pltpu.CompilerParams(collective_id=0, has_side_effects=True),
        name="attribution",
    )(
        tokens,
        step_index.reshape(1, 1),
        rate_log.reshape(1, 1),
        decay_bias.reshape(1, 1),
        beta_bias.reshape(1, 1),
        gain_one.reshape(1, width),
        gain_two.reshape(1, width),
        decay_weight.reshape(1, width),
        beta_weight.reshape(1, width),
        embed_table.reshape(words // 8, 8, slab),
        gate_weight.T,
        up_weight.T,
        down_weight,
        query_weight,
        key_weight,
        value_weight,
        cotangent,
    )
    return attribution.T


def solution(mesh):
    placed = (
        P("outer"), P(), P(None, "inner"), P(), P(None, "inner"), P(None, "inner"),
        P("inner", None), P(), P(None, "inner"), P(None, "inner"), P(None, "inner"),
        P(None, "inner"), P(None, "inner"), P("inner"), P("inner"), P("inner"),
        P("outer", "inner"),
    )
    return jax.shard_map(
        shards, mesh=mesh, in_specs=placed, out_specs=P("outer", "inner"), check_vma=False
    )
```

time: 144 us -> 105 us (0.73)
  the two profiles are of different devices: /device:TPU:232 before, /device:TPU:2 now
where the time goes in v2:
time: 105 us; the launch traced here: 104 us
  Pallas kernels  99.4 us (95%)
  between operations  2.59 us (2%)
  local copies, waits for them, and re-layouts  1.74 us (2%)
    pallas_call x1, Pallas kernels, shards(): pl.pallas_call(functools.partial(kernel, chips), out_shape=jax.ShapeDtype...  99.4 us

profile of v2, /device:TPU:2, one launch (start us, length us, event | category | flops | bytes accessed | tf_op | source)
XLA Modules:
  0.0 103.8 jit_solution(2948945659429528227)
XLA Ops:
  2.6 99.4 %attribution.1 = f32[352,256]{1,0:T(8,128)} custom-call(s32[256]{0:T(256)} %tokens_ref.1, s32[1,1]{1,0:T(1,128)} %bitcast.12.step_ref, f32[1,1]{1,0:T(1,128)} %bitcast.13.rate_ref, f32[1,1]{1,0:T(1,128)} %bitcast.14.decay_bias_ref, f32[1,1]{1,0:T(1,128)} %bitcast.15.beta_bias_ref, f32[1,2048]{1,0:T(1,128)} %bitcast.20, f32[1,2048]{1,0:T(1,128)} %bitcast.21, ...), custom_call_target="tpu_custom_call" | custom-call | tf_op jit(solution)/shard_map/attribution/pallas_call | solution.py:512
  102.0 1.7 %copy.23 = f32[256,352]{0,1:T(8,128)} copy(f32[256,352]{0,1:T(8,128)} %bitcast.17) | data formatting | bytes 720896

commit v3 on v2

--- a/solution.py
+++ b/solution.py
@@ -45,6 +45,13 @@
         return lax.dot_general(one, two, dims, preferred_element_type=F32)
 
     return dot(left_high, right_high) + (dot(left_high, right_low) + dot(left_low, right_high))
+
+
+def times(left, right):
+    high, low = split(left)
+    return jnp.dot(high, right, preferred_element_type=F32) + jnp.dot(
+        low, right, preferred_element_type=F32
+    )
 
 
 near = triple
@@ -173,8 +180,9 @@
     table, gate_w, up_w, down_w, main_w, cot_v, gates_w, emb, normed, hidden, part,
     heap_one, heap_two, sums, last_one, last_two,
     normed_two, grad_mixed, mixed_own, pair_map_out, pair_map_in, pair_off_out,
-    pair_off_in, carry_in, carry_out, share_out, share_in,
-    load_sem, send_sem, recv_sem, side_send, side_recv,
+    pair_off_in, until_map, until_off, through_map, through_off, level_map_out, level_map_in,
+    level_off_out, level_off_in, share_out, share_in,
+    load_sem, send_sem, recv_sem, side_send, side_recv, level_send, level_recv,
 ):
     me = lax.axis_index("inner")
     outer = lax.axis_index("outer")
@@ -183,10 +191,8 @@
     line, spot = me // side, lax.rem(me, side)
     chip, core = outer // 2, lax.rem(outer, 2)
     partner = {"outer": outer + 1 - 2 * core}
-    ahead = {"outer": lax.rem(chip + 1, chips) * 2 + core}
-    behind = {"outer": lax.rem(chip + chips - 1, chips) * 2 + core}
     turn = chip + core * (chips - 1 - 2 * chip)
-    onward = {"outer": lax.rem(chip + chips + 1 - 2 * core, chips) * 2 + core}
+    toward = 1 - 2 * core
 
     key_dim = query_hbm.shape[1]
     value_dim = value_hbm.shape[1]
@@ -215,7 +221,9 @@
             line * side + lax.rem(spot + step, side),
         ):
             pl.semaphore_signal(barrier, inc=1, device_id={"inner": peer}, device_id_type=MESH)
-    for device in (partner, ahead, behind):
+    pl.semaphore_signal(barrier, inc=1, device_id=partner, device_id_type=MESH)
+    for step in range(1, chips):
+        device = {"outer": lax.rem(chip + step, chips) * 2 + core}
         pl.semaphore_signal(barrier, inc=1, device_id=device, device_id_type=MESH)
     for load in loads:
         load.start()
@@ -248,7 +256,7 @@
         return carry
 
     lax.fori_loop(0, rows // 16, pick, 0)
-    pl.semaphore_wait(barrier, 2 * (side - 1) + 3)
+    pl.semaphore_wait(barrier, 2 * (side - 1) + chips)
 
     def to_axis(across, step):
         if across:
@@ -431,27 +439,68 @@
         copy.start()
     for copy in pair_copies:
         copy.wait()
-    chip_map = exact(pair_map_in[...], own_map)
-    chip_off = exact(pair_map_in[...], own_off) + pair_off_in[...].astype(F32)
-
-    pass_on = to_side(2, carry_out, carry_in, onward)
-
-    @pl.when(turn == 0)
-    def _():
-        carry_in[...] = jnp.zeros_like(carry_in)
-
-    @pl.when(turn > 0)
-    def _():
-        pass_on.wait_recv()
-
-    @pl.when(turn < chips - 1)
-    def _():
-        carry_out[...] = (exact(chip_map, carry_in[...].astype(F32)) + chip_off).astype(BF16)
-        pass_on.start()
-
-    carried = carry_in[...].astype(F32)
-    share_out[...] = (exact(own_map, carried) + own_off).astype(BF16)
-    swap = to_side(3, share_out, share_in, partner)
+    through_map[...] = triple(pair_map_in[...], own_map)
+    through_off[...] = triple(pair_map_in[...], own_off) + pair_off_in[...].astype(F32)
+    until_map[...] = (
+        lax.broadcasted_iota(jnp.int32, until_map.shape, 0)
+        == lax.broadcasted_iota(jnp.int32, until_map.shape, 1)
+    ).astype(F32)
+    until_off[...] = jnp.zeros_like(until_off)
+
+    levels = chips.bit_length() - 1
+
+    def level_copy(kind, level, step):
+        out, into = ((level_off_out, level_off_in), (level_map_out, level_map_in))[kind]
+        return pltpu.make_async_remote_copy(
+            src_ref=out.at[level],
+            dst_ref=into.at[level],
+            send_sem=level_send.at[kind, 2**level - 1 + step - 1],
+            recv_sem=level_recv.at[kind, level],
+            device_id={"outer": lax.rem(chip + toward * step + chips, chips) * 2 + core},
+            device_id_type=MESH,
+        )
+
+    for level in range(levels):
+        span = 2 ** level
+        final = level == levels - 1
+        place = lax.rem(turn, 2 * span)
+        leading = turn < 2 * span
+
+        @pl.when(place == span - 1)
+        def _():
+            level_off_out[level] = through_off[...].astype(BF16)
+            if not final:
+                level_map_out[level] = through_map[...].astype(BF16)
+            for step in range(span, 0, -1):
+                if not final:
+                    @pl.when(jnp.logical_not(leading))
+                    def _():
+                        level_copy(1, level, step).start()
+                level_copy(0, level, step).start()
+
+        @pl.when(place >= span)
+        def _():
+            if not final:
+                @pl.when(jnp.logical_not(leading))
+                def _():
+                    level_copy(1, level, 1).wait_recv()
+            level_copy(0, level, 1).wait_recv()
+            got = level_off_in[level]
+            until_off[...] = until_off[...] + times(until_map[...], got)
+            if not final:
+                @pl.when(place == 2 * span - 1)
+                def _():
+                    through_off[...] = through_off[...] + times(through_map[...], got)
+
+                @pl.when(jnp.logical_not(leading))
+                def _():
+                    got_map = level_map_in[level]
+                    until_map[...] = times(until_map[...], got_map)
+                    through_map[...] = times(through_map[...], got_map)
+
+    carried = until_off[...]
+    share_out[...] = (triple(own_map, carried) + own_off).astype(BF16)
+    swap = to_side(2, share_out, share_in, partner)
     swap.start()
     swap.wait()
     other = share_in[...].astype(F32)
@@ -459,9 +508,17 @@
     end_grad = jnp.where(first, other, carried)
     d_query, d_key, d_value, d_decay, d_beta = delta_finish(kept, state, end_grad)
 
-    @pl.when(turn < chips - 1)
-    def _():
-        pass_on.wait_send()
+    for level in range(levels):
+        span = 2 ** level
+
+        @pl.when(lax.rem(turn, 2 * span) == span - 1)
+        def _():
+            for step in range(span, 0, -1):
+                level_copy(0, level, step).wait_send()
+                if level < levels - 1:
+                    @pl.when(jnp.logical_not(turn < 2 * span))
+                    def _():
+                        level_copy(1, level, step).wait_send()
 
     grads = jnp.concatenate([d_query, d_key, d_value], axis=1).astype(BF16)
     d_decay = d_decay.astype(BF16).astype(F32)
@@ -508,6 +565,7 @@
     in_place = pl.BlockSpec(memory_space=pl.ANY)
     vm = pltpu.VMEM
     messages = (side + 1) * (side - 1)
+    levels = chips.bit_length() - 1
     state = (key_dim, value_dim)
     attribution = pl.pallas_call(
         functools.partial(kernel, chips),
@@ -538,15 +596,23 @@
             vm((key_dim, key_dim), F32),
             vm(state, BF16),
             vm(state, BF16),
-            vm(state, BF16),
-            vm(state, BF16),
+            vm((key_dim, key_dim), F32),
+            vm(state, F32),
+            vm((key_dim, key_dim), F32),
+            vm(state, F32),
+            vm((levels, key_dim, key_dim), BF16),
+            vm((levels, key_dim, key_dim), BF16),
+            vm((levels,) + state, BF16),
+            vm((levels,) + state, BF16),
             vm(state, BF16),
             vm(state, BF16),
             pltpu.SemaphoreType.DMA((8,)),
             pltpu.SemaphoreType.DMA((5, 2, messages)),
             pltpu.SemaphoreType.DMA((5, 2, messages)),
-            pltpu.SemaphoreType.DMA((4,)),
-            pltpu.SemaphoreType.DMA((4,)),
+            pltpu.SemaphoreType.DMA((3,)),
+            pltpu.SemaphoreType.DMA((3,)),
+            pltpu.SemaphoreType.DMA((2, chips - 1)),
+            pltpu.SemaphoreType.DMA((2, levels)),
         ],
         compiler_params=pltpu.CompilerParams(collective_id=0, has_side_effects=True),
         name="attribution",

time: 105 us -> 95.8 us (0.912)
  Pallas kernels: 99.4 us -> 91 us
    pallas_call x1, Pallas kernels: 99.4 us -> 91 us  [shards(): pl.pallas_call(functools.partial(kernel, chips), out_shape=jax.ShapeDtype...]
where the time goes in v3:
time: 95.8 us; the launch traced here: 95.4 us
  Pallas kernels  91 us (95%)
  between operations  2.59 us (3%)
  local copies, waits for them, and re-layouts  1.74 us (2%)
    pallas_call x1, Pallas kernels, shards(): pl.pallas_call(functools.partial(kernel, chips), out_shape=jax.ShapeDtype...  91 us

profile of v3, /device:TPU:2, one launch (start us, length us, event | category | flops | bytes accessed | tf_op | source)
XLA Modules:
  0.0 95.4 jit_solution(5643915029177581338)
XLA Ops:
  2.6 91.0 %attribution.1 = f32[352,256]{1,0:T(8,128)} custom-call(s32[256]{0:T(256)} %tokens_ref.1, s32[1,1]{1,0:T(1,128)} %bitcast.12.step_ref, f32[1,1]{1,0:T(1,128)} %bitcast.13.rate_ref, f32[1,1]{1,0:T(1,128)} %bitcast.14.decay_bias_ref, f32[1,1]{1,0:T(1,128)} %bitcast.15.beta_bias_ref, f32[1,2048]{1,0:T(1,128)} %bitcast.20, f32[1,2048]{1,0:T(1,128)} %bitcast.21, ...), custom_call_target="tpu_custom_call" | custom-call | tf_op jit(solution)/shard_map/attribution/pallas_call | solution.py:570
  93.6 1.7 %copy.23 = f32[256,352]{0,1:T(8,128)} copy(f32[256,352]{0,1:T(8,128)} %bitcast.17) | data formatting | bytes 720896

commit v4 on v3

--- a/solution.py
+++ b/solution.py
@@ -54,23 +54,39 @@
     )
 
 
-near = triple
+def running(ones, column):
+    wide = jnp.broadcast_to(column, (column.shape[0], 128))
+    high, rest = wide.astype(BF16), wide
+    total = None
+    for _ in range(3):
+        high = rest.astype(BF16)
+        rest = rest - high.astype(F32)
+        term = jnp.dot(ones, high, preferred_element_type=F32)
+        total = term if total is None else total + term
+    return total
+
+
+near = fast
 solve = triple
 gram = triple
 
 
-def unit_inverse(lower, rows, cols):
+def unit_inverse(lower):
     size = lower.shape[0]
-    eye = (rows == cols).astype(F32)
-    inverse, span = eye, 1
-    while span < size:
-        joined = (rows // (2 * span) == cols // (2 * span)) & (rows // span != cols // span)
-        below = jnp.where(joined, lower, 0.0)
-        if span == 1:
-            inverse = eye - below
-        else:
-            inverse = inverse - solve(inverse, solve(below, inverse))
-        span *= 2
+    if size > 128:
+        middle = size // 2
+        upper_left = unit_inverse(lower[:middle, :middle])
+        lower_right = unit_inverse(lower[middle:, middle:])
+        below = -solve(lower_right, solve(lower[middle:, :middle], upper_left))
+        top = jnp.concatenate([upper_left, jnp.zeros_like(below)], axis=1)
+        return jnp.concatenate([top, jnp.concatenate([below, lower_right], axis=1)], axis=0)
+    apart = lax.broadcasted_iota(jnp.int32, (size, size), 0) ^ lax.broadcasted_iota(
+        jnp.int32, (size, size), 1
+    )
+    inverse = jnp.where(apart == 0, 1.0, 0.0) - jnp.where(apart == 1, lower, 0.0)
+    for level in range(1, size.bit_length() - 1):
+        joined = jnp.where(lax.shift_right_logical(apart, level) == 1, lower, 0.0)
+        inverse = inverse - solve(inverse, solve(joined, inverse))
     return inverse
 
 
@@ -88,9 +104,9 @@
     rows = lax.broadcasted_iota(jnp.int32, (size, size), 0)
     cols = lax.broadcasted_iota(jnp.int32, (size, size), 1)
     lower = rows >= cols
-    ones_lower = lower.astype(F32)
-    cum_rows = exact(ones_lower, jnp.broadcast_to(log_decay, (size, size)))
-    cum_cols = cum_rows.T
+    cum_wide = running(lower.astype(F32).astype(BF16), log_decay)
+    cum_rows = jnp.concatenate([cum_wide] * (size // 128), axis=1)
+    cum_cols = jnp.concatenate([cum_wide.T] * (size // 128), axis=0)
     ratio = jnp.where(lower, jnp.exp(jnp.where(lower, cum_rows - cum_cols, 0.0)), 0.0)
     cum = cum_rows[:, 0:1]
     cum_last = cum_cols[:, size - 1 : size]
@@ -101,7 +117,7 @@
     key_gram = gram(keys, keys, NT)
     ratio_gram = jnp.where(rows > cols, ratio * key_gram, 0.0)
     strict = betas * ratio_gram
-    inverse = unit_inverse(strict, rows, cols)
+    inverse = unit_inverse(strict)
     scores = ratio * near(queries, keys, NT)
     keys_grown = grown * keys
     queries_grown = grown * queries
@@ -153,8 +169,8 @@
     ends = jnp.sum(row_sum(k["keys"] * fresh_end), axis=0, keepdims=True) + k["total"] * jnp.sum(
         row_sum(state * end_grad), axis=0, keepdims=True
     )
-    upper = (rows <= cols).astype(F32)
-    d_log = exact(upper, jnp.broadcast_to(d_cum, (size, key_dim)))[:, 0:1] + ends
+    upper = (rows <= cols).astype(F32).astype(BF16)
+    d_log = running(upper, d_cum)[:, 0:1] + ends
 
     query_inv, key_inv = k["query_inv"], k["key_inv"]
     d_query = (scale * query_inv) * (
@@ -173,16 +189,16 @@
 
 def kernel(
     chips,
-    tokens_ref, step_ref, rate_ref, decay_bias_ref, beta_bias_ref, gain_one_ref, gain_two_ref,
-    decay_ref, beta_ref, table_hbm, gate_hbm, up_hbm, down_hbm, query_hbm, key_hbm, value_hbm,
+    tokens_hbm, step_ref, rate_ref, decay_bias_ref, beta_bias_ref, gain_one_hbm, gain_two_hbm,
+    decay_hbm, beta_hbm, table_hbm, gate_hbm, up_hbm, down_hbm, query_hbm, key_hbm, value_hbm,
     cot_hbm,
     out_ref,
-    table, gate_w, up_w, down_w, main_w, cot_v, gates_w, emb, normed, hidden, part,
+    tokens_ref, gain_one_ref, gain_two_ref, decay_ref, beta_ref, table, gate_w, up_w, down_w, main_w, cot_v, gates_w, emb, normed, hidden, part,
     heap_one, heap_two, sums, last_one, last_two,
     normed_two, grad_mixed, mixed_own, pair_map_out, pair_map_in, pair_off_out,
-    pair_off_in, until_map, until_off, through_map, through_off, level_map_out, level_map_in,
+    pair_off_in, until_map, until_off, share_map, share_off, through_map, through_off, level_map_out, level_map_in,
     level_off_out, level_off_in, share_out, share_in,
-    load_sem, send_sem, recv_sem, side_send, side_recv, level_send, level_recv,
+    small_sem, load_sem, send_sem, recv_sem, side_send, side_recv, level_send, level_recv,
 ):
     me = lax.axis_index("inner")
     outer = lax.axis_index("outer")
@@ -202,6 +218,26 @@
     share = rows // peers
     slab = table.shape[2]
 
+    barrier = pltpu.get_barrier_semaphore()
+    for step in range(1, side):
+        for peer in (
+            lax.rem(line + step, side) * side + spot,
+            line * side + lax.rem(spot + step, side),
+        ):
+            pl.semaphore_signal(barrier, inc=1, device_id={"inner": peer}, device_id_type=MESH)
+    pl.semaphore_signal(barrier, inc=1, device_id=partner, device_id_type=MESH)
+    for step in range(1, chips):
+        device = {"outer": lax.rem(chip + step, chips) * 2 + core}
+        pl.semaphore_signal(barrier, inc=1, device_id=device, device_id_type=MESH)
+
+    small = [
+        pltpu.make_async_copy(source, target, small_sem.at[index])
+        for index, (source, target) in enumerate((
+            (tokens_hbm, tokens_ref), (gain_one_hbm, gain_one_ref), (gain_two_hbm, gain_two_ref),
+            (decay_hbm, decay_ref), (beta_hbm, beta_ref),
+        ))
+    ]
+    small[0].start()
     loads = [
         pltpu.make_async_copy(gate_hbm, gate_w, load_sem.at[0]),
         pltpu.make_async_copy(up_hbm, up_w, load_sem.at[1]),
@@ -213,21 +249,13 @@
     ]
     table_load = pltpu.make_async_copy(table_hbm, table, load_sem.at[7])
     table_load.start()
-
-    barrier = pltpu.get_barrier_semaphore()
-    for step in range(1, side):
-        for peer in (
-            lax.rem(line + step, side) * side + spot,
-            line * side + lax.rem(spot + step, side),
-        ):
-            pl.semaphore_signal(barrier, inc=1, device_id={"inner": peer}, device_id_type=MESH)
-    pl.semaphore_signal(barrier, inc=1, device_id=partner, device_id_type=MESH)
-    for step in range(1, chips):
-        device = {"outer": lax.rem(chip + step, chips) * 2 + core}
-        pl.semaphore_signal(barrier, inc=1, device_id=device, device_id_type=MESH)
+    for load in small[1:]:
+        load.start()
     for load in loads:
         load.start()
 
+    for load in small:
+        load.wait()
     row_id = lax.broadcasted_iota(jnp.int32, (8, width), 0)
     gates_w[...] = jnp.where(
         row_id == 0,
@@ -367,7 +395,7 @@
     gate_rows = lax.dot_general(normed[...], gate_w[...], NT, preferred_element_type=F32)
     up_rows = lax.dot_general(normed[...], up_w[...], NT, preferred_element_type=F32)
     active = gate_rows * (1.0 / (1.0 + jnp.exp(-gate_rows))) * up_rows
-    path_scale = (step_ref[...].astype(F32) + 0.5) / STEPS
+    path_scale = (step_ref[0].astype(F32) + 0.5) / STEPS
     scaled = (path_scale * active).astype(BF16)
     loads[2].wait()
 
@@ -410,9 +438,9 @@
         gates[:, 0:1],
         gates[:, 1:2],
         cot_v[...].astype(F32),
-        rate_ref[...],
-        decay_bias_ref[...],
-        beta_bias_ref[...],
+        jnp.full((1, 1), rate_ref[0]),
+        decay_bias_ref[0],
+        beta_bias_ref[0],
     )
 
     first = core == 0
@@ -460,6 +488,17 @@
             device_id_type=MESH,
         )
 
+    def extend_until(level):
+        span = 2**level
+
+        @pl.when(lax.rem(turn, 2 * span) >= span)
+        def _():
+            until_off[...] = until_off[...] + times(until_map[...], level_off_in[level])
+            if level < levels - 1:
+                @pl.when(turn >= 2 * span)
+                def _():
+                    until_map[...] = times(until_map[...], level_map_in[level])
+
     for level in range(levels):
         span = 2 ** level
         final = level == levels - 1
@@ -478,6 +517,12 @@
                         level_copy(1, level, step).start()
                 level_copy(0, level, step).start()
 
+        if level > 0:
+            extend_until(level - 1)
+        if final:
+            share_map[...] = triple(own_map, until_map[...])
+            share_off[...] = triple(own_map, until_off[...]) + own_off
+
         @pl.when(place >= span)
         def _():
             if not final:
@@ -486,23 +531,23 @@
                     level_copy(1, level, 1).wait_recv()
             level_copy(0, level, 1).wait_recv()
             got = level_off_in[level]
-            until_off[...] = until_off[...] + times(until_map[...], got)
-            if not final:
+            if final:
+                share_off[...] = share_off[...] + times(share_map[...], got)
+            else:
                 @pl.when(place == 2 * span - 1)
                 def _():
                     through_off[...] = through_off[...] + times(through_map[...], got)
 
-                @pl.when(jnp.logical_not(leading))
-                def _():
-                    got_map = level_map_in[level]
-                    until_map[...] = times(until_map[...], got_map)
-                    through_map[...] = times(through_map[...], got_map)
-
-    carried = until_off[...]
-    share_out[...] = (triple(own_map, carried) + own_off).astype(BF16)
+                    @pl.when(jnp.logical_not(leading))
+                    def _():
+                        through_map[...] = times(through_map[...], level_map_in[level])
+
+    share_out[...] = share_off[...].astype(BF16)
     swap = to_side(2, share_out, share_in, partner)
     swap.start()
+    extend_until(levels - 1)
     swap.wait()
+    carried = until_off[...]
     other = share_in[...].astype(F32)
     state = jnp.where(first, carried, other)
     end_grad = jnp.where(first, other, carried)
@@ -570,9 +615,14 @@
     attribution = pl.pallas_call(
         functools.partial(kernel, chips),
         out_shape=jax.ShapeDtypeStruct((hidden_dim, rows), F32),
-        in_specs=[in_smem] + [in_vmem] * 8 + [in_place] * 8,
+        in_specs=[in_place] + [in_smem] * 4 + [in_place] * 12,
         out_specs=in_vmem,
         scratch_shapes=[
+            pltpu.SMEM((rows,), jnp.int32),
+            vm((1, width), F32),
+            vm((1, width), F32),
+            vm((1, width), BF16),
+            vm((1, width), BF16),
             vm((words // 8, 8, slab), BF16),
             vm((hidden_dim, width), BF16),
             vm((hidden_dim, width), BF16),
@@ -600,12 +650,15 @@
             vm(state, F32),
             vm((key_dim, key_dim), F32),
             vm(state, F32),
+            vm((key_dim, key_dim), F32),
+            vm(state, F32),
             vm((levels, key_dim, key_dim), BF16),
             vm((levels, key_dim, key_dim), BF16),
             vm((levels,) + state, BF16),
             vm((levels,) + state, BF16),
             vm(state, BF16),
             vm(state, BF16),
+            pltpu.SemaphoreType.DMA((5,)),
             pltpu.SemaphoreType.DMA((8,)),
             pltpu.SemaphoreType.DMA((5, 2, messages)),
             pltpu.SemaphoreType.DMA((5, 2, messages)),
@@ -618,10 +671,10 @@
         name="attribution",
     )(
         tokens,
-        step_index.reshape(1, 1),
-        rate_log.reshape(1, 1),
-        decay_bias.reshape(1, 1),
-        beta_bias.reshape(1, 1),
+        step_index,
+        rate_log,
+        decay_bias,
+        beta_bias,
         gain_one.reshape(1, width),
         gain_two.reshape(1, width),
         decay_weight.reshape(1, width),

time: 95.8 us -> 93.8 us (0.979)
  Pallas kernels: 91 us -> 89.3 us
    pallas_call x1, Pallas kernels: 91 us -> 89.3 us  [shards(): pl.pallas_call(functools.partial(kernel, chips), out_shape=jax.ShapeDtype...]
where the time goes in v4:
time: 93.8 us; the launch traced here: 93.6 us
  Pallas kernels  89.3 us (95%)
  between operations  2.59 us (3%)
  local copies, waits for them, and re-layouts  1.74 us (2%)
    pallas_call x1, Pallas kernels, shards(): pl.pallas_call(functools.partial(kernel, chips), out_shape=jax.ShapeDtype...  89.3 us

profile of v4, /device:TPU:2, one launch (start us, length us, event | category | flops | bytes accessed | tf_op | source)
XLA Modules:
  0.0 93.6 jit_solution(17830198514077978339)
XLA Ops:
  2.6 89.3 %attribution.1 = f32[352,256]{1,0:T(8,128)} custom-call(s32[256]{0:T(256)} %tokens_hbm.1, s32[1]{0:T(128)S(6)} %copy.19.step_ref, f32[1]{0:T(128)S(6)} %copy.20.rate_ref, f32[1]{0:T(128)S(6)} %copy.21.decay_bias_ref, f32[1]{0:T(128)S(6)} %copy.22.beta_bias_ref, f32[1,2048]{1,0:T(1,128)} %bitcast.12, f32[1,2048]{1,0:T(1,128)} %bitcast.13, ...), custom_call_target="tpu_custom_call" | custom-call | tf_op jit(solution)/shard_map/attribution/pallas_call | solution.py:615
  91.9 1.7 %copy.23 = f32[256,352]{0,1:T(8,128)} copy(f32[256,352]{0,1:T(8,128)} %bitcast.9) | data formatting | bytes 720896

commit v5 on v4

--- a/solution.py
+++ b/solution.py
@@ -51,6 +51,13 @@
     high, low = split(left)
     return jnp.dot(high, right, preferred_element_type=F32) + jnp.dot(
         low, right, preferred_element_type=F32
+    )
+
+
+def apply(left, right):
+    high, low = split(right)
+    return jnp.dot(left, high, preferred_element_type=F32) + jnp.dot(
+        left, low, preferred_element_type=F32
     )
 
 
@@ -123,10 +130,10 @@
     queries_grown = grown * queries
     keys_tail = left_over * keys
 
-    fresh_free = near(inverse, betas * values)
-    fresh_map = near(inverse, betas * keys_grown)
-    back_free = near(inverse, near(scores, cot, TN), TN)
-    back_map = near(inverse, keys_tail, TN)
+    fresh_free = solve(inverse, betas * values)
+    fresh_map = solve(inverse, betas * keys_grown)
+    back_free = solve(inverse, near(scores, cot, TN), TN)
+    back_map = solve(inverse, keys_tail, TN)
     eye = (
         lax.broadcasted_iota(jnp.int32, (key_dim, key_dim), 0)
         == lax.broadcasted_iota(jnp.int32, (key_dim, key_dim), 1)
@@ -196,9 +203,10 @@
     tokens_ref, gain_one_ref, gain_two_ref, decay_ref, beta_ref, table, gate_w, up_w, down_w, main_w, cot_v, gates_w, emb, normed, hidden, part,
     heap_one, heap_two, sums, last_one, last_two,
     normed_two, grad_mixed, mixed_own, pair_map_out, pair_map_in, pair_off_out,
-    pair_off_in, until_map, until_off, share_map, share_off, through_map, through_off, level_map_out, level_map_in,
-    level_off_out, level_off_in, share_out, share_in,
-    small_sem, load_sem, send_sem, recv_sem, side_send, side_recv, level_send, level_recv,
+    pair_off_in, until_map, until_off, share_map, share_off, through_map, through_off, map_out, map_in,
+    off_out, off_in, middle_out, middle_in, share_out, share_in,
+    small_sem, load_sem, send_sem, recv_sem, side_send, side_recv, group_send, group_recv,
+    middle_send, middle_recv,
 ):
     me = lax.axis_index("inner")
     outer = lax.axis_index("outer")
@@ -475,77 +483,91 @@
     ).astype(F32)
     until_off[...] = jnp.zeros_like(until_off)
 
-    levels = chips.bit_length() - 1
-
-    def level_copy(kind, level, step):
-        out, into = ((level_off_out, level_off_in), (level_map_out, level_map_in))[kind]
+    group = chips // 2
+    place = lax.rem(turn, group)
+    early = turn < group
+    map_out[...] = through_map[...].astype(BF16)
+    off_out[...] = through_off[...].astype(BF16)
+
+    def along(step):
+        return {"outer": lax.rem(chip + toward * step + chips, chips) * 2 + core}
+
+    def group_copy(kind, apart):
+        out, into = ((off_out, off_in), (map_out, map_in))[kind]
         return pltpu.make_async_remote_copy(
-            src_ref=out.at[level],
-            dst_ref=into.at[level],
-            send_sem=level_send.at[kind, 2**level - 1 + step - 1],
-            recv_sem=level_recv.at[kind, level],
-            device_id={"outer": lax.rem(chip + toward * step + chips, chips) * 2 + core},
+            src_ref=out,
+            dst_ref=into.at[apart - 1],
+            send_sem=group_send.at[kind, apart - 1],
+            recv_sem=group_recv.at[kind, apart - 1],
+            device_id=along(apart),
             device_id_type=MESH,
         )
 
-    def extend_until(level):
-        span = 2**level
-
-        @pl.when(lax.rem(turn, 2 * span) >= span)
+    def middle_copy(step):
+        return pltpu.make_async_remote_copy(
+            src_ref=middle_out,
+            dst_ref=middle_in,
+            send_sem=middle_send.at[step - 1],
+            recv_sem=middle_recv.at[0],
+            device_id=along(step),
+            device_id_type=MESH,
+        )
+
+    for apart in range(group - 1, 0, -1):
+        @pl.when(place + apart < group)
         def _():
-            until_off[...] = until_off[...] + times(until_map[...], level_off_in[level])
-            if level < levels - 1:
-                @pl.when(turn >= 2 * span)
+            @pl.when(turn > 0)
+            def _():
+                group_copy(1, apart).start()
+            group_copy(0, apart).start()
+
+    for apart in range(group - 1, 0, -1):
+        @pl.when(place >= apart)
+        def _():
+            @pl.when(turn > apart)
+            def _():
+                group_copy(1, apart).wait_recv()
+            group_copy(0, apart).wait_recv()
+
+            @pl.when(place == apart)
+            def _():
+                until_off[...] = off_in[apart - 1].astype(F32)
+
+                @pl.when(jnp.logical_not(early))
                 def _():
-                    until_map[...] = times(until_map[...], level_map_in[level])
-
-    for level in range(levels):
-        span = 2 ** level
-        final = level == levels - 1
-        place = lax.rem(turn, 2 * span)
-        leading = turn < 2 * span
-
-        @pl.when(place == span - 1)
-        def _():
-            level_off_out[level] = through_off[...].astype(BF16)
-            if not final:
-                level_map_out[level] = through_map[...].astype(BF16)
-            for step in range(span, 0, -1):
-                if not final:
-                    @pl.when(jnp.logical_not(leading))
-                    def _():
-                        level_copy(1, level, step).start()
-                level_copy(0, level, step).start()
-
-        if level > 0:
-            extend_until(level - 1)
-        if final:
-            share_map[...] = triple(own_map, until_map[...])
-            share_off[...] = triple(own_map, until_off[...]) + own_off
-
-        @pl.when(place >= span)
-        def _():
-            if not final:
-                @pl.when(jnp.logical_not(leading))
+                    until_map[...] = map_in[apart - 1].astype(F32)
+
+            @pl.when(place > apart)
+            def _():
+                got_map = map_in[apart - 1]
+                until_off[...] = apply(got_map, until_off[...]) + off_in[apart - 1].astype(F32)
+
+                @pl.when(jnp.logical_not(early))
                 def _():
-                    level_copy(1, level, 1).wait_recv()
-            level_copy(0, level, 1).wait_recv()
-            got = level_off_in[level]
-            if final:
-                share_off[...] = share_off[...] + times(share_map[...], got)
-            else:
-                @pl.when(place == 2 * span - 1)
-                def _():
-                    through_off[...] = through_off[...] + times(through_map[...], got)
-
-                    @pl.when(jnp.logical_not(leading))
-                    def _():
-                        through_map[...] = times(through_map[...], level_map_in[level])
+                    until_map[...] = apply(got_map, until_map[...])
+
+    @pl.when(turn == group - 1)
+    def _():
+        middle_out[...] = (triple(through_map[...], until_off[...]) + through_off[...]).astype(BF16)
+        for step in range(group, 0, -1):
+            middle_copy(step).start()
+
+    share_map[...] = triple(own_map, until_map[...])
+    share_off[...] = triple(own_map, until_off[...]) + own_off
+
+    @pl.when(turn >= group)
+    def _():
+        middle_copy(1).wait_recv()
+        share_off[...] = share_off[...] + times(share_map[...], middle_in[...])
 
     share_out[...] = share_off[...].astype(BF16)
     swap = to_side(2, share_out, share_in, partner)
     swap.start()
-    extend_until(levels - 1)
+
+    @pl.when(turn >= group)
+    def _():
+        until_off[...] = until_off[...] + times(until_map[...], middle_in[...])
+
     swap.wait()
     carried = until_off[...]
     other = share_in[...].astype(F32)
@@ -553,17 +575,18 @@
     end_grad = jnp.where(first, other, carried)
     d_query, d_key, d_value, d_decay, d_beta = delta_finish(kept, state, end_grad)
 
-    for level in range(levels):
-        span = 2 ** level
-
-        @pl.when(lax.rem(turn, 2 * span) == span - 1)
+    for apart in range(group - 1, 0, -1):
+        @pl.when(place + apart < group)
         def _():
-            for step in range(span, 0, -1):
-                level_copy(0, level, step).wait_send()
-                if level < levels - 1:
-                    @pl.when(jnp.logical_not(turn < 2 * span))
-                    def _():
-                        level_copy(1, level, step).wait_send()
+            @pl.when(turn > 0)
+            def _():
+                group_copy(1, apart).wait_send()
+            group_copy(0, apart).wait_send()
+
+    @pl.when(turn == group - 1)
+    def _():
+        for step in range(group, 0, -1):
+            middle_copy(step).wait_send()
 
     grads = jnp.concatenate([d_query, d_key, d_value], axis=1).astype(BF16)
     d_decay = d_decay.astype(BF16).astype(F32)
@@ -610,7 +633,7 @@
     in_place = pl.BlockSpec(memory_space=pl.ANY)
     vm = pltpu.VMEM
     messages = (side + 1) * (side - 1)
-    levels = chips.bit_length() - 1
+    group = chips // 2
     state = (key_dim, value_dim)
     attribution = pl.pallas_call(
         functools.partial(kernel, chips),
@@ -652,10 +675,12 @@
             vm(state, F32),
             vm((key_dim, key_dim), F32),
             vm(state, F32),
-            vm((levels, key_dim, key_dim), BF16),
-            vm((levels, key_dim, key_dim), BF16),
-            vm((levels,) + state, BF16),
-            vm((levels,) + state, BF16),
+            vm((key_dim, key_dim), BF16),
+            vm((group - 1, key_dim, key_dim), BF16),
+            vm(state, BF16),
+            vm((group - 1,) + state, BF16),
+            vm(state, BF16),
+            vm(state, BF16),
             vm(state, BF16),
             vm(state, BF16),
             pltpu.SemaphoreType.DMA((5,)),
@@ -664,8 +689,10 @@
             pltpu.SemaphoreType.DMA((5, 2, messages)),
             pltpu.SemaphoreType.DMA((3,)),
             pltpu.SemaphoreType.DMA((3,)),
-            pltpu.SemaphoreType.DMA((2, chips - 1)),
-            pltpu.SemaphoreType.DMA((2, levels)),
+            pltpu.SemaphoreType.DMA((2, group - 1)),
+            pltpu.SemaphoreType.DMA((2, group - 1)),
+            pltpu.SemaphoreType.DMA((group,)),
+            pltpu.SemaphoreType.DMA((1,)),
         ],
         compiler_params=pltpu.CompilerParams(collective_id=0, has_side_effects=True),
         name="attribution",

time: 93.8 us -> 94.9 us (1.012)
  Pallas kernels: 89.3 us -> 90.4 us
    pallas_call x1, Pallas kernels: 89.3 us -> 90.4 us  [shards(): pl.pallas_call(functools.partial(kernel, chips), out_shape=jax.ShapeDtype...]
where the time goes in v5:
time: 94.9 us; the launch traced here: 94.7 us
  Pallas kernels  90.4 us (95%)
  between operations  2.59 us (3%)
  local copies, waits for them, and re-layouts  1.74 us (2%)
    pallas_call x1, Pallas kernels, shards(): pl.pallas_call(functools.partial(kernel, chips), out_shape=jax.ShapeDtype...  90.4 us

profile of v5, /device:TPU:2, one launch (start us, length us, event | category | flops | bytes accessed | tf_op | source)
XLA Modules:
  0.0 94.7 jit_solution(17870371146565271261)
XLA Ops:
  2.6 90.4 %attribution.1 = f32[352,256]{1,0:T(8,128)} custom-call(s32[256]{0:T(256)} %tokens_hbm.1, s32[1]{0:T(128)S(6)} %copy.19.step_ref, f32[1]{0:T(128)S(6)} %copy.20.rate_ref, f32[1]{0:T(128)S(6)} %copy.21.decay_bias_ref, f32[1]{0:T(128)S(6)} %copy.22.beta_bias_ref, f32[1,2048]{1,0:T(1,128)} %bitcast.12, f32[1,2048]{1,0:T(1,128)} %bitcast.13, ...), custom_call_target="tpu_custom_call" | custom-call | tf_op jit(solution)/shard_map/attribution/pallas_call | solution.py:638
  93.0 1.7 %copy.23 = f32[256,352]{0,1:T(8,128)} copy(f32[256,352]{0,1:T(8,128)} %bitcast.9) | data formatting | bytes 720896
